TPU v7x, 32 devices: a whole 2x2x4 slice. The times are simulated.
32 devices in a mesh: dp: 8 (over z, y), section: 4 (over x, core).
Axes of the slice: x: 2, y: 2, z: 4, core: 2. Of those that a mesh axis runs over, the one named last changes fastest.
Arguments:
- inputs: bfloat16 [32, 532, 768], P(('dp', 'section')), may hold values from -6 to 6
- qkv_weight: bfloat16 [2, 768, 2304], replicated, may hold values from -0.21875 to 0.21875
- query_bias: bfloat16 [2, 768], replicated, may hold values from -3 to 3
- value_bias: bfloat16 [2, 768], replicated, may hold values from -0.59765625 to 0.59765625
- out_weight: bfloat16 [2, 768, 768], replicated, may hold values from -1.75 to 1.75
- out_bias: bfloat16 [2, 768], replicated, may hold values from -3 to 3
- norm1_gain: bfloat16 [2, 768], replicated, may hold values from 0.25 to 1.75
- norm1_shift: bfloat16 [2, 768], replicated, may hold values from -3 to 3
- up_weight: bfloat16 [2, 768, 3072], replicated, may hold values from -0.21875 to 0.21875
- up_bias: bfloat16 [2, 3072], replicated, may hold values from -3 to 3
- down_weight: bfloat16 [2, 3072, 768], replicated, may hold values from -0.109375 to 0.109375
- down_bias: bfloat16 [2, 768], replicated, may hold values from -3 to 3
- norm2_gain: bfloat16 [2, 768], replicated, may hold values from 0.25 to 1.75
- norm2_shift: bfloat16 [2, 768], replicated, may hold values from -3 to 3
- cotangent: bfloat16 [32, 80, 768], P(('dp', 'section')), may hold values from -6 to 6
- masked_rows: int32 [32, 80], P(('dp', 'section')), may hold values from 10 to 521
- row_valid: int32 [32, 80], P(('dp', 'section')), may hold values 0 or 1
Outputs:
- masked_out: bfloat16 [32, 80, 768], P(('dp', 'section'))
- input_grad: float32 [32, 532, 768], P(('dp', 'section'))
- grad_qkv: float32 [2, 768, 2304], P(None, 'dp')
- grad_query_bias: float32 [2, 768], P(None, 'dp')
- grad_value_bias: float32 [2, 768], P(None, 'dp')
- grad_out_weight: float32 [2, 768, 768], P(None, 'dp')
- grad_out_bias: float32 [2, 768], P(None, 'dp')
- grad_norm1_gain: float32 [2, 768], P(None, 'dp')
- grad_norm1_shift: float32 [2, 768], P(None, 'dp')
- grad_up_weight: float32 [2, 768, 3072], P(None, 'dp')
- grad_up_bias: float32 [2, 3072], P(None, 'dp')
- grad_down_weight: float32 [2, 3072, 768], P(None, 'dp')
- grad_down_bias: float32 [2, 768], P(None, 'dp')
- grad_norm2_gain: float32 [2, 768], P(None, 'dp')
- grad_norm2_shift: float32 [2, 768], P(None, 'dp')
All inputs are finite; a program needn't handle non-finite values. No bound on the sum of `row_valid` on one device may be relied on, other than what follows from the above.
Results may differ from a plain program's by a relative error of at most 0.023.
Values may be sent and summed in bfloat16 or wider, within the bound.
No kernel may reach another device: no remote copies, remote signals or barrier semaphores. Data moves between devices by JAX's collectives and lax.ppermute only.
A program may use at most 320 MiB of HBM per device.

v0:
```python
import jax
import jax.numpy as jnp
from jax import lax
from jax.sharding import PartitionSpec as P

HEAD_DIM = 64


EPS = 1e-06


def from_behind(value, axis, steps):
    count = lax.axis_size(axis)
    leading, last = (max(0, -steps), min(count, count - steps))
    return lax.ppermute(value, axis, [(source, source + steps) for source in range(leading, last)])


def layer_norm(resid, norm_gain, norm_shift):
    centre = jnp.mean(resid, -1, keepdims=True)
    offset = resid - centre
    spread = jnp.mean(offset * offset, -1, keepdims=True)
    return offset * lax.rsqrt(spread + EPS) * norm_gain + norm_shift


def exact_gelu(pre_values):
    return jax.nn.gelu(pre_values, approximate=False)


def take_block(stacked, index_now):
    return lax.dynamic_index_in_dim(stacked, index_now, 0, keepdims=False)


def add_pair(first_term, second_term):
    return first_term + second_term


def layer_pieces(hidden, params):
    (
        qkv_weight,
        query_bias,
        value_bias,
        out_weight,
        out_bias,
        norm1_gain,
        norm1_shift,
        up_weight,
        up_bias,
        down_weight,
        down_bias,
        norm2_gain,
        norm2_shift,
    ) = params
    row_count, model_width = hidden.shape
    head_count = model_width // HEAD_DIM
    score_scale = HEAD_DIM ** (-0.5)
    projected = jnp.dot(hidden, qkv_weight, preferred_element_type=jnp.float32)
    queries = (
        (projected[:, :model_width] + query_bias)
        .astype(jnp.bfloat16)
        .reshape(row_count, head_count, HEAD_DIM)
    )
    key_rows = (
        projected[:, model_width : 2 * model_width]
        .astype(jnp.bfloat16)
        .reshape(row_count, head_count, HEAD_DIM)
    )
    value_rows = (
        (projected[:, 2 * model_width :] + value_bias)
        .astype(jnp.bfloat16)
        .reshape(row_count, head_count, HEAD_DIM)
    )
    scores = (
        jnp.einsum("qhd,khd->hqk", queries, key_rows, preferred_element_type=jnp.float32)
        * score_scale
    )
    softmax_out = jax.nn.softmax(scores, axis=-1)
    softmax_low = softmax_out.astype(jnp.bfloat16)
    attended = jnp.einsum(
        "hqk,khd->qhd", softmax_low, value_rows, preferred_element_type=jnp.float32
    )
    attended = attended.reshape(row_count, model_width).astype(jnp.bfloat16)
    first_sum = hidden.astype(jnp.float32) + (
        jnp.dot(attended, out_weight, preferred_element_type=jnp.float32) + out_bias
    )
    first_norm = layer_norm(first_sum, norm1_gain, norm1_shift)
    first_low = first_norm.astype(jnp.bfloat16)
    up_pre = jnp.dot(first_low, up_weight, preferred_element_type=jnp.float32) + up_bias
    activated = exact_gelu(up_pre).astype(jnp.bfloat16)
    second_sum = first_norm + (
        jnp.dot(activated, down_weight, preferred_element_type=jnp.float32) + down_bias
    )
    layer_out = layer_norm(second_sum, norm2_gain, norm2_shift)
    return (
        queries,
        key_rows,
        value_rows,
        softmax_out,
        softmax_low,
        attended,
        first_sum,
        first_low,
        up_pre,
        activated,
        second_sum,
        layer_out,
    )


def layer_backward(hidden, params, grad_out):
    (
        qkv_weight,
        query_bias,
        value_bias,
        out_weight,
        out_bias,
        norm1_gain,
        norm1_shift,
        up_weight,
        up_bias,
        down_weight,
        down_bias,
        norm2_gain,
        norm2_shift,
    ) = params
    (
        queries,
        key_rows,
        value_rows,
        softmax_out,
        softmax_low,
        attended,
        first_sum,
        first_low,
        up_pre,
        activated,
        second_sum,
        layer_out,
    ) = layer_pieces(hidden, params)
    row_count, model_width = hidden.shape
    head_count = model_width // HEAD_DIM
    score_scale = HEAD_DIM ** (-0.5)
    second_vjp = jax.vjp(layer_norm, second_sum, norm2_gain, norm2_shift)[1]
    d_second, grad_norm2_gain, grad_norm2_shift = second_vjp(grad_out)
    d_down = d_second.astype(jnp.bfloat16)
    grad_down_bias = jnp.sum(d_down.astype(jnp.float32), 0)
    grad_down_weight = jnp.einsum(
        "rf,rd->fd", activated, d_down, preferred_element_type=jnp.float32
    )
    d_active = jnp.einsum("rd,fd->rf", d_down, down_weight, preferred_element_type=jnp.float32)
    gelu_vjp = jax.vjp(exact_gelu, up_pre)[1]
    d_up = gelu_vjp(d_active)[0].astype(jnp.bfloat16)
    grad_up_bias = jnp.sum(d_up.astype(jnp.float32), 0)
    grad_up_weight = jnp.einsum("rd,rf->df", first_low, d_up, preferred_element_type=jnp.float32)
    d_first_norm = d_second + jnp.einsum(
        "rf,df->rd", d_up, up_weight, preferred_element_type=jnp.float32
    )
    first_vjp = jax.vjp(layer_norm, first_sum, norm1_gain, norm1_shift)[1]
    d_first, grad_norm1_gain, grad_norm1_shift = first_vjp(d_first_norm)
    d_branch = d_first.astype(jnp.bfloat16)
    grad_out_bias = jnp.sum(d_branch.astype(jnp.float32), 0)
    grad_out_weight = jnp.einsum(
        "ra,rd->ad", attended, d_branch, preferred_element_type=jnp.float32
    )
    d_attended = jnp.einsum("rd,ad->ra", d_branch, out_weight, preferred_element_type=jnp.float32)
    d_attended = d_attended.astype(jnp.bfloat16).reshape(row_count, head_count, HEAD_DIM)
    d_softmax = jnp.einsum(
        "qhd,khd->hqk", d_attended, value_rows, preferred_element_type=jnp.float32
    )
    d_values = jnp.einsum(
        "hqk,qhd->khd", softmax_low, d_attended, preferred_element_type=jnp.float32
    )
    d_values = d_values.astype(jnp.bfloat16).reshape(row_count, model_width)
    row_terms = jnp.sum(softmax_out * d_softmax, -1, keepdims=True)
    d_scores = (softmax_out * (d_softmax - row_terms)).astype(jnp.bfloat16)
    d_queries = (
        jnp.einsum("hqk,khd->qhd", d_scores, key_rows, preferred_element_type=jnp.float32)
        * score_scale
    )
    d_queries = d_queries.astype(jnp.bfloat16).reshape(row_count, model_width)
    d_keys = (
        jnp.einsum("hqk,qhd->khd", d_scores, queries, preferred_element_type=jnp.float32)
        * score_scale
    )
    d_keys = d_keys.astype(jnp.bfloat16).reshape(row_count, model_width)
    d_project = jnp.concatenate([d_queries, d_keys, d_values], 1)
    grad_query_bias = jnp.sum(d_queries.astype(jnp.float32), 0)
    grad_value_bias = jnp.sum(d_values.astype(jnp.float32), 0)
    grad_qkv = jnp.einsum("rd,re->de", hidden, d_project, preferred_element_type=jnp.float32)
    d_hidden = d_first + jnp.einsum(
        "re,de->rd", d_project, qkv_weight, preferred_element_type=jnp.float32
    )
    return (
        d_hidden,
        (
            grad_qkv,
            grad_query_bias,
            grad_value_bias,
            grad_out_weight,
            grad_out_bias,
            grad_norm1_gain,
            grad_norm1_shift,
            grad_up_weight,
            grad_up_bias,
            grad_down_weight,
            grad_down_bias,
            grad_norm2_gain,
            grad_norm2_shift,
        ),
    )


def local(
    inputs,
    qkv_weight,
    query_bias,
    value_bias,
    out_weight,
    out_bias,
    norm1_gain,
    norm1_shift,
    up_weight,
    up_bias,
    down_weight,
    down_bias,
    norm2_gain,
    norm2_shift,
    cotangent,
    masked_rows,
    row_valid,
):
    half_section = lax.axis_size("section") // 2
    section_id = lax.axis_index("section")
    layer_id = section_id // half_section
    leading = layer_id == 0
    stacks = (
        qkv_weight,
        query_bias,
        value_bias,
        out_weight,
        out_bias,
        norm1_gain,
        norm1_shift,
        up_weight,
        up_bias,
        down_weight,
        down_bias,
        norm2_gain,
        norm2_shift,
    )
    params = tuple(
        (
            (
                take_block(stacked, layer_id)
                if stacked.ndim == 3
                else take_block(stacked, layer_id).astype(jnp.float32)
            )
            for stacked in stacks
        )
    )
    own_segments, row_count, model_width = inputs.shape
    micro_count = 2 * own_segments
    partner_inputs = from_behind(inputs, "section", -half_section)
    pipe_inputs = jnp.concatenate([inputs, partner_inputs], 0)
    positions = jnp.arange(row_count, dtype=jnp.int32)
    selector = (
        (masked_rows[:, :, None] == positions).astype(jnp.float32)
        * row_valid[:, :, None].astype(jnp.float32)
    ).astype(jnp.bfloat16)
    prior_cot, prior_sel = from_behind((cotangent, selector), "section", half_section)
    pipe_cot = jnp.concatenate([prior_cot, cotangent], 0)
    pipe_sel = jnp.concatenate([prior_sel, selector], 0)

    def forward_tick(incoming, tick_index):
        fresh_rows = take_block(pipe_inputs, jnp.minimum(tick_index, micro_count - 1))
        current = jnp.where(leading, fresh_rows, incoming)
        result = layer_pieces(current, params)[-1].astype(jnp.bfloat16)
        passed = from_behind(result, "section", half_section)
        chosen = take_block(pipe_sel, jnp.maximum(tick_index - 1, 0))
        gathered = jnp.dot(chosen, result, preferred_element_type=jnp.float32).astype(jnp.bfloat16)
        return (passed, (gathered, passed))

    tick_list = jnp.arange(micro_count + 1, dtype=jnp.int32)
    start_rows = jnp.zeros((row_count, model_width), jnp.bfloat16)
    final_rows, (gathered_all, received) = lax.scan(forward_tick, start_rows, tick_list)
    returned_out = from_behind(gathered_all[1 : 1 + own_segments], "section", -half_section)
    masked_out = jnp.where(leading, returned_out, gathered_all[1 + own_segments :])
    zero_totals = tuple((jnp.zeros(piece.shape, jnp.float32) for piece in params))

    def backward_tick(state_in, tick_index):
        incoming, totals = state_in
        upper_index = jnp.minimum(tick_index, micro_count - 1)
        lower_index = jnp.maximum(tick_index - 1, 0)
        fresh_rows = take_block(pipe_inputs, upper_index)
        recomputed = layer_pieces(fresh_rows, params)[-1].astype(jnp.bfloat16)
        upper_input = from_behind(recomputed, "section", half_section)
        lower_input = take_block(pipe_inputs, lower_index)
        current = jnp.where(leading, lower_input, upper_input)
        top_grad = jnp.einsum(
            "mr,md->rd",
            take_block(pipe_sel, upper_index),
            take_block(pipe_cot, upper_index),
            preferred_element_type=jnp.float32,
        )
        grad_out = jnp.where(leading, incoming.astype(jnp.float32), top_grad)
        grad_in, grads = layer_backward(current, params, grad_out)
        active = jnp.where(leading, tick_index >= 1, tick_index < micro_count)
        grads = tuple((jnp.where(active, piece, 0.0) for piece in grads))
        sent_back = from_behind(grad_in.astype(jnp.bfloat16), "section", -half_section)
        totals = tuple(
            (add_pair(first_term, second_term) for first_term, second_term in zip(totals, grads))
        )
        return ((sent_back, totals), grad_in)

    (final_grad, totals), grad_inputs = lax.scan(
        backward_tick, (start_rows, zero_totals), tick_list
    )
    reduced = (
        lax.psum_scatter(totals[0], "dp", scatter_dimension=0, tiled=True),
        lax.psum_scatter(totals[1], "dp", scatter_dimension=0, tiled=True),
        lax.psum_scatter(totals[2], "dp", scatter_dimension=0, tiled=True),
        lax.psum_scatter(totals[3], "dp", scatter_dimension=0, tiled=True),
        lax.psum_scatter(totals[4], "dp", scatter_dimension=0, tiled=True),
        lax.psum_scatter(totals[5], "dp", scatter_dimension=0, tiled=True),
        lax.psum_scatter(totals[6], "dp", scatter_dimension=0, tiled=True),
        lax.psum_scatter(totals[7], "dp", scatter_dimension=0, tiled=True),
        lax.psum_scatter(totals[8], "dp", scatter_dimension=0, tiled=True),
        lax.psum_scatter(totals[9], "dp", scatter_dimension=0, tiled=True),
        lax.psum_scatter(totals[10], "dp", scatter_dimension=0, tiled=True),
        lax.psum_scatter(totals[11], "dp", scatter_dimension=0, tiled=True),
        lax.psum_scatter(totals[12], "dp", scatter_dimension=0, tiled=True),
    )

    def slot_pair(piece):
        return jnp.stack(
            [jnp.where(layer_id == 0, piece, 0.0), jnp.where(layer_id == 1, piece, 0.0)]
        )

    slots = tuple((slot_pair(piece) for piece in reduced))
    summed = (
        lax.psum(slots[0].astype(jnp.bfloat16), "section").astype(jnp.float32),
        lax.psum(slots[1].astype(jnp.bfloat16), "section").astype(jnp.float32),
        lax.psum(slots[2].astype(jnp.bfloat16), "section").astype(jnp.float32),
        lax.psum(slots[3].astype(jnp.bfloat16), "section").astype(jnp.float32),
        lax.psum(slots[4].astype(jnp.bfloat16), "section").astype(jnp.float32),
        lax.psum(slots[5].astype(jnp.bfloat16), "section").astype(jnp.float32),
        lax.psum(slots[6].astype(jnp.bfloat16), "section").astype(jnp.float32),
        lax.psum(slots[7].astype(jnp.bfloat16), "section").astype(jnp.float32),
        lax.psum(slots[8].astype(jnp.bfloat16), "section").astype(jnp.float32),
        lax.psum(slots[9].astype(jnp.bfloat16), "section").astype(jnp.float32),
        lax.psum(slots[10].astype(jnp.bfloat16), "section").astype(jnp.float32),
        lax.psum(slots[11].astype(jnp.bfloat16), "section").astype(jnp.float32),
        lax.psum(slots[12].astype(jnp.bfloat16), "section").astype(jnp.float32),
    )
    returned_grad = from_behind(
        grad_inputs[1 + own_segments :].astype(jnp.bfloat16), "section", half_section
    ).astype(jnp.float32)
    input_grad = jnp.where(leading, grad_inputs[1 : 1 + own_segments], returned_grad)
    return (
        masked_out,
        input_grad,
        summed[0],
        summed[1],
        summed[2],
        summed[3],
        summed[4],
        summed[5],
        summed[6],
        summed[7],
        summed[8],
        summed[9],
        summed[10],
        summed[11],
        summed[12],
    )


def solution(mesh):
    return jax.shard_map(
        local,
        mesh=mesh,
        in_specs=(
            P(("dp", "section"), None, None),
            P(),
            P(),
            P(),
            P(),
            P(),
            P(),
            P(),
            P(),
            P(),
            P(),
            P(),
            P(),
            P(),
            P(("dp", "section"), None, None),
            P(("dp", "section"), None),
            P(("dp", "section"), None),
        ),
        out_specs=(
            P(("dp", "section"), None, None),
            P(("dp", "section"), None, None),
            P(None, "dp", None),
            P(None, "dp"),
            P(None, "dp"),
            P(None, "dp", None),
            P(None, "dp"),
            P(None, "dp"),
            P(None, "dp"),
            P(None, "dp", None),
            P(None, "dp"),
            P(None, "dp", None),
            P(None, "dp"),
            P(None, "dp"),
            P(None, "dp"),
        ),
        check_vma=False,
    )
```

profile of v0, /device:TPU:0, one launch (start us, length us, event | category | flops | bytes accessed | tf_op | source)
XLA Modules:
  0.0 1381.5 jit_solution(17526046276218017512)
XLA Ops:
  39.3 715.6 %while.56 = (s32[]{:T(128)}, bf16[532,768]{1,0:T(8,128)(2,1)}, f32[768,2304]{1,0:T(8,128)}, f32[768]{0:T(1024)}, f32[768]{0:T(1024)}, /*index=5*/f32[768,768]{1,...) while((s32[]{:T(128)}, bf16[532,768]{1,0:T(8,128)(2,1)}, ...), condition=%wide.region_35.36_spmd.clone, body=%wide.region_8.35_spmd.clone.sunk | while | flops 34059694080 | bytes 640240768 | solution.py:314
  49.5 9.8 fusion.444
  59.3 7.5 fusion.445
  70.1 23.5 %fusion.447 = (f32[532]{0:T(1024)S(1)}, f32[532,768]{1,0:T(8,128)S(1)}) fusion(f32[768]{0:T(1024)S(1)} %get-tuple-element.1686, bf16[3072,768]{1,0:T(8,128)(2,1)} %get-tuple-element.1685, bf16[768,3072]{1,0:T(8,128)(2,1)} %get-tuple-element.1683, f32[3072]{0:T(1024)S(1)} %get-tuple-element.1684, f32[532,768]{1,0:T(8,128)} %copy-done.10, ...), kind=kOutput, calls=%fused_computation.397.clone.1 | convolution fusion | flops 5133348352 | bytes 12733680 | tf_op jit(solution)/shard_map/while/body/eval_jaxpr/dot_general | solution.py:90
  97.9 15.0 %collective-permute-done.1 = bf16[532,768]{1,0:T(8,128)(2,1)S(1)} collective-permute-done((bf16[532,768]{1,0:T(8,128)(2,1)S(1)}, bf16[532,768]{1,0:T(8,128)(2,1)S(1)}, u32[]{:S(2)}, u32[]{:S(2)}) %collective-permute-start.1) | collective-permute-done | bytes 817184 | tf_op jit(solution)/shard_map/while/body/eval_jaxpr/ppermute | solution.py:15
  121.8 8.5 fusion.450
  130.3 7.6 fusion.451
  139.3 20.9 %multiply_convert_fusion.7 = (bf16[532,3072]{1,0:T(8,128)(2,1)S(1)}, f32[532,3072]{1,0:T(8,128)}, f32[532,3072]{1,0:T(8,128)}) fusion(f32[3072]{0:T(1024)S(1)} %get-tuple-element.1684, bf16[768,3072]{1,0:T(8,128)(2,1)} %get-tuple-element.1683, f32[532,768]{1,0:T(8,128)S(1)} %get-tuple-element.1453, f32[532]{0:T(1024)S(1)} %fusion.453, ...), kind=kOutput, calls=%fused_computation.115.clone.1 | convolution fusion | flops 2620197888 | bytes 22718624 | tf_op jit(solution)/shard_map/while/body/eval_jaxpr/dot_general | solution.py:87
  165.5 9.7 convert_reduce_fusion.11
  186.9 9.8 convert_reduce_fusion.13
  196.6 10.5 multiply_reduce_fusion.31
  207.1 11.3 multiply_convert_fusion.8
  228.9 7.0 select_add_fusion.27
  235.9 5.7 select_add_fusion.29
  253.8 7.4 select_add_fusion.22
  261.3 10.2 collective-permute-done.2
  282.6 10.0 fusion.444
  292.6 7.5 fusion.445
  303.5 23.3 %fusion.447 = (f32[532]{0:T(1024)S(1)}, f32[532,768]{1,0:T(8,128)S(1)}) fusion(f32[768]{0:T(1024)S(1)} %get-tuple-element.1686, bf16[3072,768]{1,0:T(8,128)(2,1)} %get-tuple-element.1685, bf16[768,3072]{1,0:T(8,128)(2,1)} %get-tuple-element.1683, f32[3072]{0:T(1024)S(1)} %get-tuple-element.1684, f32[532,768]{1,0:T(8,128)} %copy-done.10, ...), kind=kOutput, calls=%fused_computation.397.clone.1 | convolution fusion | flops 5133348352 | bytes 12733680 | tf_op jit(solution)/shard_map/while/body/eval_jaxpr/dot_general | solution.py:90
  330.9 13.5 collective-permute-done.1
  353.4 8.5 fusion.450
  361.9 7.6 fusion.451
  370.9 21.1 %multiply_convert_fusion.7 = (bf16[532,3072]{1,0:T(8,128)(2,1)S(1)}, f32[532,3072]{1,0:T(8,128)}, f32[532,3072]{1,0:T(8,128)}) fusion(f32[3072]{0:T(1024)S(1)} %get-tuple-element.1684, bf16[768,3072]{1,0:T(8,128)(2,1)} %get-tuple-element.1683, f32[532,768]{1,0:T(8,128)S(1)} %get-tuple-element.1453, f32[532]{0:T(1024)S(1)} %fusion.453, ...), kind=kOutput, calls=%fused_computation.115.clone.1 | convolution fusion | flops 2620197888 | bytes 22718624 | tf_op jit(solution)/shard_map/while/body/eval_jaxpr/dot_general | solution.py:87
  397.3 9.7 convert_reduce_fusion.11
  418.4 9.8 convert_reduce_fusion.13
  428.2 10.5 multiply_reduce_fusion.31
  438.7 11.3 multiply_convert_fusion.8
  461.2 9.5 select_add_fusion.27
  470.7 5.7 select_add_fusion.29
  488.5 9.4 select_add_fusion.22
  498.0 6.9 collective-permute-done.2
  516.2 9.7 fusion.444
  525.9 7.5 fusion.445
  536.8 23.3 %fusion.447 = (f32[532]{0:T(1024)S(1)}, f32[532,768]{1,0:T(8,128)S(1)}) fusion(f32[768]{0:T(1024)S(1)} %get-tuple-element.1686, bf16[3072,768]{1,0:T(8,128)(2,1)} %get-tuple-element.1685, bf16[768,3072]{1,0:T(8,128)(2,1)} %get-tuple-element.1683, f32[3072]{0:T(1024)S(1)} %get-tuple-element.1684, f32[532,768]{1,0:T(8,128)} %copy-done.10, ...), kind=kOutput, calls=%fused_computation.397.clone.1 | convolution fusion | flops 5133348352 | bytes 12733680 | tf_op jit(solution)/shard_map/while/body/eval_jaxpr/dot_general | solution.py:90
  564.3 12.1 collective-permute-done.1
  585.4 8.5 fusion.450
  593.9 7.6 fusion.451
  602.9 20.9 %multiply_convert_fusion.7 = (bf16[532,3072]{1,0:T(8,128)(2,1)S(1)}, f32[532,3072]{1,0:T(8,128)}, f32[532,3072]{1,0:T(8,128)}) fusion(f32[3072]{0:T(1024)S(1)} %get-tuple-element.1684, bf16[768,3072]{1,0:T(8,128)(2,1)} %get-tuple-element.1683, f32[532,768]{1,0:T(8,128)S(1)} %get-tuple-element.1453, f32[532]{0:T(1024)S(1)} %fusion.453, ...), kind=kOutput, calls=%fused_computation.115.clone.1 | convolution fusion | flops 2620197888 | bytes 22718624 | tf_op jit(solution)/shard_map/while/body/eval_jaxpr/dot_general | solution.py:87
  629.1 9.7 convert_reduce_fusion.11
  650.3 9.8 convert_reduce_fusion.13
  660.1 10.5 multiply_reduce_fusion.31
  670.5 11.3 multiply_convert_fusion.8
  693.0 9.7 select_add_fusion.27
  702.8 5.7 select_add_fusion.29
  712.3 5.4 fusion.458
  720.6 9.4 select_add_fusion.22
  758.8 209.2 %while.55 = (s32[]{:T(128)}, bf16[532,768]{1,0:T(8,128)(2,1)S(1)}, bf16[3,80,768]{2,1,0:T(8,128)(2,1)}, pred[]{:T(512)}, s32[3]{0:T(128)S(1)}, /*index=5*/bf16[2...) while((s32[]{:T(128)}, bf16[532,768]{1,0:T(8,128)(2,1)S(1)}, ...), condition=%wide.region_7.8_spmd, body=%wide.region_0.7_spmd.sunk | while | flops 8604494848 | bytes 97890568 | solution.py:284
  768.3 9.6 fusion.395
  777.9 7.7 fusion.396
  788.9 23.2 %fusion.398 = (f32[532]{0:T(1024)S(1)}, f32[532,768]{1,0:T(8,128)S(1)}) fusion(f32[768]{0:T(1024)S(1)} %get-tuple-element.1562, bf16[3072,768]{1,0:T(8,128)(2,1)} %get-tuple-element.1561, bf16[768,3072]{1,0:T(8,128)(2,1)} %get-tuple-element.1559, f32[3072]{0:T(1024)S(1)} %get-tuple-element.1560, f32[532,768]{1,0:T(8,128)} %copy-done.9, ...), kind=kOutput, calls=%fused_computation.394.clone.1 | convolution fusion | flops 5133348352 | bytes 12733680 | tf_op jit(solution)/shard_map/while/body/eval_jaxpr/dot_general | solution.py:90
  816.3 10.9 collective-permute-done
  836.7 9.6 fusion.395
  846.3 7.7 fusion.396
  857.4 23.3 %fusion.398 = (f32[532]{0:T(1024)S(1)}, f32[532,768]{1,0:T(8,128)S(1)}) fusion(f32[768]{0:T(1024)S(1)} %get-tuple-element.1562, bf16[3072,768]{1,0:T(8,128)(2,1)} %get-tuple-element.1561, bf16[768,3072]{1,0:T(8,128)(2,1)} %get-tuple-element.1559, f32[3072]{0:T(1024)S(1)} %get-tuple-element.1560, f32[532,768]{1,0:T(8,128)} %copy-done.9, ...), kind=kOutput, calls=%fused_computation.394.clone.1 | convolution fusion | flops 5133348352 | bytes 12733680 | tf_op jit(solution)/shard_map/while/body/eval_jaxpr/dot_general | solution.py:90
  887.6 10.1 collective-permute-done
  907.1 9.6 fusion.395
  916.8 7.5 fusion.396
  927.9 23.1 %fusion.398 = (f32[532]{0:T(1024)S(1)}, f32[532,768]{1,0:T(8,128)S(1)}) fusion(f32[768]{0:T(1024)S(1)} %get-tuple-element.1562, bf16[3072,768]{1,0:T(8,128)(2,1)} %get-tuple-element.1561, bf16[768,3072]{1,0:T(8,128)(2,1)} %get-tuple-element.1559, f32[3072]{0:T(1024)S(1)} %get-tuple-element.1560, f32[532,768]{1,0:T(8,128)} %copy-done.9, ...), kind=kOutput, calls=%fused_computation.394.clone.1 | convolution fusion | flops 5133348352 | bytes 12733680 | tf_op jit(solution)/shard_map/while/body/eval_jaxpr/dot_general | solution.py:90
  957.9 10.0 collective-permute-done
  976.5 40.9 %all-reduce.9 = (bf16[768]{0:T(1024)(128)(2,1)S(1)}, bf16[768]{0:T(1024)(128)(2,1)S(1)}, bf16[768]{0:T(1024)(128)(2,1)S(1)}, bf16[768]{0:T(1024)(128)(2,1)S(1)},...) all-reduce(f32[768]{0:T(1024)S(1)} %copy-done.75, ...), channel_id=3, replica_groups=mesh['dp'=8,'section'=4] {'dp'}, use_global_device_ids=true, to_apply=%region_38.39.clone | all-reduce | flops 9216 | bytes 55296
  1021.5 102.0 %reduce-scatter.9.cloned.1.call-done = f32[96,3072]{1,0:T(8,128)} async-done(((f32[768,3072]{1,0:T(8,128)}), f32[96,3072]{1,0:T(8,128)}) %reduce-scatter.9.cloned.1.call-update) | async-done | bytes 1179664 | tf_op jit(solution)/shard_map/reduce_scatter | solution.py:325
  1126.1 162.1 %reduce-scatter.11.cloned.1.call-done = f32[384,768]{1,0:T(8,128)} async-done(((f32[3072,768]{1,0:T(8,128)}), f32[384,768]{1,0:T(8,128)}) %reduce-scatter.11.cloned.1.call-update) | async-done | bytes 1179664 | tf_op jit(solution)/shard_map/reduce_scatter | solution.py:327
  1291.2 6.5 all-reduce.10
  1308.9 57.0 %all-reduce.14.cloned.1.call-done = (bf16[2,96,2304]{2,1,0:T(8,128)(2,1)}, bf16[2,96,768]{2,1,0:T(8,128)(2,1)}, bf16[2,96,3072]{2,1,0:T(8,128)(2,1)}, bf16[2,384,768]{2,1,0:T(8,128)(2,1)}) async-done(((bf16[2,96,2304]{2,1,0:T(8,128)(2,1)}, bf16[2,96,768]{2,1,0:T(8,128)(2,1)}, bf16[2,96,3072]{2,1,0:T(8,128)(2,1)}, bf16[2,384,768]{2,1,0:T(8,128)(2,1)}), (bf16[2,96,2304]{2,1,0:T(8,128)(2,1)}, ...) | async-done | bytes 3538960 | tf_op jit(solution)/shard_map/psum | solution.py:340
  (803 shorter events, 320.0 us)
Async XLA Ops:
  7.2 1010.3 %reduce-scatter.7.cloned.1.call-start = ((), (), s32[]{:S(2)}) async-start(), calls=%async_computation.5 | async-start | bytes 2654208 | tf_op jit(solution)/shard_map/reduce_scatter | solution.py:321
  8.8 23.6 %collective-permute-start.4 = (bf16[1,80,532]{2,1,0:T(8,128)(2,1)S(1)}, bf16[1,80,532]{2,1,0:T(8,128)(2,1)S(1)}, u32[]{:S(2)}, u32[]{:S(2)}) collective-permute-start(bf16[1,80,532]{2,1,0:T(8,128)(2,1)S(1)} %select_convert_fusion.8), channel_id=1, source_target_pairs={{0,2},{1,3},{4,6},{5,7},{8,10},{9,11},{12,14},{13,15},{16,18},{17,... | collective-permute-start | bytes 255368 | tf_op jit(solution)/shard_map/ppermute | solution.py:15
  13.7 19.4 %collective-permute-start.6 = (bf16[1,80,768]{2,1,0:T(8,128)(2,1)}, bf16[1,80,768]{2,1,0:T(8,128)(2,1)S(1)}, u32[]{:S(2)}, u32[]{:S(2)}) collective-permute-start(bf16[1,80,768]{2,1,0:T(8,128)(2,1)} %param.35), channel_id=1, source_target_pairs={{0,2},{1,3},{4,6},{5,7},{8,10},{9,11},{12,14},{13,15},{16,18},{17,... | collective-permute-start | bytes 368648 | tf_op jit(solution)/shard_map/ppermute | solution.py:15
  15.0 21.9 %collective-permute-start.3 = (bf16[1,532,768]{2,1,0:T(8,128)(2,1)}, bf16[1,532,768]{2,1,0:T(8,128)(2,1)S(1)}, u32[]{:S(2)}, u32[]{:S(2)}) collective-permute-start(bf16[1,532,768]{2,1,0:T(8,128)(2,1)} %param.21), channel_id=1, source_target_pairs={{2,0},{3,1},{6,4},{7,5},{10,8},{11,9},{14,12},{15,13},{18,16},{19,... | collective-permute-start | bytes 2451464 | tf_op jit(solution)/shard_map/ppermute | solution.py:15
  39.5 54.5 %copy-start.44 = (f32[768]{0:T(1024)}, f32[768]{0:T(1024)S(1)}, u32[]{:S(2)}) copy-start(f32[768]{0:T(1024)S(1)} %get-tuple-element.1687) | copy-start | bytes 9220 | tf_op jit(solution)/shard_map/while
  39.5 79.2 %copy-start.32 = (f32[768]{0:T(1024)}, f32[768]{0:T(1024)S(1)}, u32[]{:S(2)}) copy-start(f32[768]{0:T(1024)S(1)} %get-tuple-element.1678) | copy-start | bytes 9220 | tf_op jit(solution)/shard_map/while
  39.5 79.2 %copy-start.36 = (f32[768]{0:T(1024)}, f32[768]{0:T(1024)S(1)}, u32[]{:S(2)}) copy-start(f32[768]{0:T(1024)S(1)} %get-tuple-element.1677) | copy-start | bytes 9220 | tf_op jit(solution)/shard_map/while
  39.5 98.4 %copy-start.77 = (f32[768]{0:T(1024)}, f32[768]{0:T(1024)S(1)}, u32[]{:S(2)}) copy-start(f32[768]{0:T(1024)S(1)} %get-tuple-element.1680) | copy-start | bytes 9220 | tf_op jit(solution)/shard_map/while
  94.3 18.6 %collective-permute-start.1 = (bf16[532,768]{1,0:T(8,128)(2,1)S(1)}, bf16[532,768]{1,0:T(8,128)(2,1)S(1)}, u32[]{:S(2)}, u32[]{:S(2)}) collective-permute-start(bf16[532,768]{1,0:T(8,128)(2,1)S(1)} %add_convert_fusion.11), channel_id=1, source_target_pairs={{0,2},{1,3},{4,6},{5,7},{8,10},{9,11},{12,14},{13,15},{16,18},{17,... | collective-permute-start | bytes 2451464 | tf_op jit(solution)/shard_map/while/body/eval_jaxpr/ppermute | solution.py:15
  137.9 22.3 %slice-start.5 = ((s8[4718592]{0:T(1024)(128)(4,1)}), s8[4194304]{0:T(1024)(128)(4,1)S(1)}, s32[]{:S(2)}) async-start(s8[4718592]{0:T(1024)(128)(4,1)} %bitcast.362), calls=%async_computation.14 | async-start | bytes 8388608 | tf_op jit(solution)/shard_map/while
  139.3 21.0 %slice-start.6 = ((s8[4718592]{0:T(1024)(128)(4,1)}), s8[524288]{0:T(1024)(128)(4,1)S(1)}, s32[]{:S(2)}) async-start(s8[4718592]{0:T(1024)(128)(4,1)} %bitcast.362), calls=%async_computation.15 | async-start | bytes 1048576 | tf_op jit(solution)/shard_map/while
  207.1 11.3 copy-start.7
  250.8 20.7 %collective-permute-start.2 = (bf16[532,768]{1,0:T(8,128)(2,1)S(1)}, bf16[532,768]{1,0:T(8,128)(2,1)S(1)}, u32[]{:S(2)}, u32[]{:S(2)}) collective-permute-start(bf16[532,768]{1,0:T(8,128)(2,1)S(1)} %get-tuple-element.1475), channel_id=1, source_target_pairs={{2,0},{3,1},{6,4},{7,5},{10,8},{11,9},{14,12},{15,13},{18,16},{19,... | collective-permute-start | bytes 2451464 | tf_op jit(solution)/shard_map/while/body/eval_jaxpr/ppermute | solution.py:15
  253.8 18.7 %copy-start.33 = (f32[768]{0:T(1024)S(1)}, f32[768]{0:T(1024)}, u32[]{:S(2)}) copy-start(f32[768]{0:T(1024)} %copy-done.32) | copy-start | bytes 9220 | tf_op jit(solution)/shard_map/while
  253.8 18.6 %copy-start.37 = (f32[768]{0:T(1024)S(1)}, f32[768]{0:T(1024)}, u32[]{:S(2)}) copy-start(f32[768]{0:T(1024)} %copy-done.36) | copy-start | bytes 9220 | tf_op jit(solution)/shard_map/while
  253.8 18.6 %copy-start.45 = (f32[768]{0:T(1024)S(1)}, f32[768]{0:T(1024)}, u32[]{:S(2)}) copy-start(f32[768]{0:T(1024)} %copy-done.44) | copy-start | bytes 9220 | tf_op jit(solution)/shard_map/while
  253.8 18.6 %copy-start.78 = (f32[768]{0:T(1024)S(1)}, f32[768]{0:T(1024)}, u32[]{:S(2)}) copy-start(f32[768]{0:T(1024)} %copy-done.77) | copy-start | bytes 9220 | tf_op jit(solution)/shard_map/while
  272.7 54.5 %copy-start.44 = (f32[768]{0:T(1024)}, f32[768]{0:T(1024)S(1)}, u32[]{:S(2)}) copy-start(f32[768]{0:T(1024)S(1)} %get-tuple-element.1687) | copy-start | bytes 9220 | tf_op jit(solution)/shard_map/while
  272.7 77.6 %copy-start.32 = (f32[768]{0:T(1024)}, f32[768]{0:T(1024)S(1)}, u32[]{:S(2)}) copy-start(f32[768]{0:T(1024)S(1)} %get-tuple-element.1678) | copy-start | bytes 9220 | tf_op jit(solution)/shard_map/while
  272.7 77.6 %copy-start.36 = (f32[768]{0:T(1024)}, f32[768]{0:T(1024)S(1)}, u32[]{:S(2)}) copy-start(f32[768]{0:T(1024)S(1)} %get-tuple-element.1677) | copy-start | bytes 9220 | tf_op jit(solution)/shard_map/while
  272.7 96.8 %copy-start.77 = (f32[768]{0:T(1024)}, f32[768]{0:T(1024)S(1)}, u32[]{:S(2)}) copy-start(f32[768]{0:T(1024)S(1)} %get-tuple-element.1680) | copy-start | bytes 9220 | tf_op jit(solution)/shard_map/while
  327.5 17.0 %collective-permute-start.1 = (bf16[532,768]{1,0:T(8,128)(2,1)S(1)}, bf16[532,768]{1,0:T(8,128)(2,1)S(1)}, u32[]{:S(2)}, u32[]{:S(2)}) collective-permute-start(bf16[532,768]{1,0:T(8,128)(2,1)S(1)} %add_convert_fusion.11), channel_id=1, source_target_pairs={{0,2},{1,3},{4,6},{5,7},{8,10},{9,11},{12,14},{13,15},{16,18},{17,... | collective-permute-start | bytes 2451464 | tf_op jit(solution)/shard_map/while/body/eval_jaxpr/ppermute | solution.py:15
  369.5 22.5 %slice-start.5 = ((s8[4718592]{0:T(1024)(128)(4,1)}), s8[4194304]{0:T(1024)(128)(4,1)S(1)}, s32[]{:S(2)}) async-start(s8[4718592]{0:T(1024)(128)(4,1)} %bitcast.362), calls=%async_computation.14 | async-start | bytes 8388608 | tf_op jit(solution)/shard_map/while
  370.9 21.2 %slice-start.6 = ((s8[4718592]{0:T(1024)(128)(4,1)}), s8[524288]{0:T(1024)(128)(4,1)S(1)}, s32[]{:S(2)}) async-start(s8[4718592]{0:T(1024)(128)(4,1)} %bitcast.362), calls=%async_computation.15 | async-start | bytes 1048576 | tf_op jit(solution)/shard_map/while
  438.7 11.3 copy-start.7
  456.6 14.1 %slice-start = ((s8[9437184]{0:T(1024)(128)(4,1)}), s8[4194304]{0:T(1024)(128)(4,1)S(1)}, s32[]{:S(2)}) async-start(s8[9437184]{0:T(1024)(128)(4,1)} %bitcast.358), calls=%async_computation.9 | async-start | bytes 8388608 | tf_op jit(solution)/shard_map/while
  485.6 19.2 %collective-permute-start.2 = (bf16[532,768]{1,0:T(8,128)(2,1)S(1)}, bf16[532,768]{1,0:T(8,128)(2,1)S(1)}, u32[]{:S(2)}, u32[]{:S(2)}) collective-permute-start(bf16[532,768]{1,0:T(8,128)(2,1)S(1)} %get-tuple-element.1475), channel_id=1, source_target_pairs={{2,0},{3,1},{6,4},{7,5},{10,8},{11,9},{14,12},{15,13},{18,16},{19,... | collective-permute-start | bytes 2451464 | tf_op jit(solution)/shard_map/while/body/eval_jaxpr/ppermute | solution.py:15
  488.5 17.3 %copy-start.33 = (f32[768]{0:T(1024)S(1)}, f32[768]{0:T(1024)}, u32[]{:S(2)}) copy-start(f32[768]{0:T(1024)} %copy-done.32) | copy-start | bytes 9220 | tf_op jit(solution)/shard_map/while
  488.5 17.3 %copy-start.37 = (f32[768]{0:T(1024)S(1)}, f32[768]{0:T(1024)}, u32[]{:S(2)}) copy-start(f32[768]{0:T(1024)} %copy-done.36) | copy-start | bytes 9220 | tf_op jit(solution)/shard_map/while
  488.5 17.3 %copy-start.45 = (f32[768]{0:T(1024)S(1)}, f32[768]{0:T(1024)}, u32[]{:S(2)}) copy-start(f32[768]{0:T(1024)} %copy-done.44) | copy-start | bytes 9220 | tf_op jit(solution)/shard_map/while
  488.5 17.2 %copy-start.78 = (f32[768]{0:T(1024)S(1)}, f32[768]{0:T(1024)}, u32[]{:S(2)}) copy-start(f32[768]{0:T(1024)} %copy-done.77) | copy-start | bytes 9220 | tf_op jit(solution)/shard_map/while
  506.2 54.3 %copy-start.44 = (f32[768]{0:T(1024)}, f32[768]{0:T(1024)S(1)}, u32[]{:S(2)}) copy-start(f32[768]{0:T(1024)S(1)} %get-tuple-element.1687) | copy-start | bytes 9220 | tf_op jit(solution)/shard_map/while
  506.2 75.9 %copy-start.32 = (f32[768]{0:T(1024)}, f32[768]{0:T(1024)S(1)}, u32[]{:S(2)}) copy-start(f32[768]{0:T(1024)S(1)} %get-tuple-element.1678) | copy-start | bytes 9220 | tf_op jit(solution)/shard_map/while
  506.2 75.9 %copy-start.36 = (f32[768]{0:T(1024)}, f32[768]{0:T(1024)S(1)}, u32[]{:S(2)}) copy-start(f32[768]{0:T(1024)S(1)} %get-tuple-element.1677) | copy-start | bytes 9220 | tf_op jit(solution)/shard_map/while
  506.2 95.3 %copy-start.77 = (f32[768]{0:T(1024)}, f32[768]{0:T(1024)S(1)}, u32[]{:S(2)}) copy-start(f32[768]{0:T(1024)S(1)} %get-tuple-element.1680) | copy-start | bytes 9220 | tf_op jit(solution)/shard_map/while
  560.8 15.5 %collective-permute-start.1 = (bf16[532,768]{1,0:T(8,128)(2,1)S(1)}, bf16[532,768]{1,0:T(8,128)(2,1)S(1)}, u32[]{:S(2)}, u32[]{:S(2)}) collective-permute-start(bf16[532,768]{1,0:T(8,128)(2,1)S(1)} %add_convert_fusion.11), channel_id=1, source_target_pairs={{0,2},{1,3},{4,6},{5,7},{8,10},{9,11},{12,14},{13,15},{16,18},{17,... | collective-permute-start | bytes 2451464 | tf_op jit(solution)/shard_map/while/body/eval_jaxpr/ppermute | solution.py:15
  601.6 22.3 %slice-start.5 = ((s8[4718592]{0:T(1024)(128)(4,1)}), s8[4194304]{0:T(1024)(128)(4,1)S(1)}, s32[]{:S(2)}) async-start(s8[4718592]{0:T(1024)(128)(4,1)} %bitcast.362), calls=%async_computation.14 | async-start | bytes 8388608 | tf_op jit(solution)/shard_map/while
  602.9 20.9 %slice-start.6 = ((s8[4718592]{0:T(1024)(128)(4,1)}), s8[524288]{0:T(1024)(128)(4,1)S(1)}, s32[]{:S(2)}) async-start(s8[4718592]{0:T(1024)(128)(4,1)} %bitcast.362), calls=%async_computation.15 | async-start | bytes 1048576 | tf_op jit(solution)/shard_map/while
  670.5 11.3 copy-start.7
  688.4 14.3 %slice-start = ((s8[9437184]{0:T(1024)(128)(4,1)}), s8[4194304]{0:T(1024)(128)(4,1)S(1)}, s32[]{:S(2)}) async-start(s8[9437184]{0:T(1024)(128)(4,1)} %bitcast.358), calls=%async_computation.9 | async-start | bytes 8388608 | tf_op jit(solution)/shard_map/while
  717.7 17.7 %collective-permute-start.2 = (bf16[532,768]{1,0:T(8,128)(2,1)S(1)}, bf16[532,768]{1,0:T(8,128)(2,1)S(1)}, u32[]{:S(2)}, u32[]{:S(2)}) collective-permute-start(bf16[532,768]{1,0:T(8,128)(2,1)S(1)} %get-tuple-element.1475), channel_id=1, source_target_pairs={{2,0},{3,1},{6,4},{7,5},{10,8},{11,9},{14,12},{15,13},{18,16},{19,... | collective-permute-start | bytes 2451464 | tf_op jit(solution)/shard_map/while/body/eval_jaxpr/ppermute | solution.py:15
  720.6 15.8 %copy-start.33 = (f32[768]{0:T(1024)S(1)}, f32[768]{0:T(1024)}, u32[]{:S(2)}) copy-start(f32[768]{0:T(1024)} %copy-done.32) | copy-start | bytes 9220 | tf_op jit(solution)/shard_map/while
  720.6 15.7 %copy-start.37 = (f32[768]{0:T(1024)S(1)}, f32[768]{0:T(1024)}, u32[]{:S(2)}) copy-start(f32[768]{0:T(1024)} %copy-done.36) | copy-start | bytes 9220 | tf_op jit(solution)/shard_map/while
  720.6 15.7 %copy-start.45 = (f32[768]{0:T(1024)S(1)}, f32[768]{0:T(1024)}, u32[]{:S(2)}) copy-start(f32[768]{0:T(1024)} %copy-done.44) | copy-start | bytes 9220 | tf_op jit(solution)/shard_map/while
  720.6 15.7 %copy-start.78 = (f32[768]{0:T(1024)S(1)}, f32[768]{0:T(1024)}, u32[]{:S(2)}) copy-start(f32[768]{0:T(1024)} %copy-done.77) | copy-start | bytes 9220 | tf_op jit(solution)/shard_map/while
  755.0 264.3 %reduce-scatter.5.cloned.1.call-start = ((), (), s32[]{:S(2)}) async-start(), calls=%async_computation.4 | async-start | bytes 7962624 | tf_op jit(solution)/shard_map/reduce_scatter | solution.py:318
  755.8 367.7 %reduce-scatter.9.cloned.1.call-start = ((), (), s32[]{:S(2)}) async-start(), calls=%async_computation.6 | async-start | bytes 10616832 | tf_op jit(solution)/shard_map/reduce_scatter | solution.py:325
  756.6 531.7 %reduce-scatter.11.cloned.1.call-start = ((), (), s32[]{:S(2)}) async-start(), calls=%async_computation.7 | async-start | bytes 10616832 | tf_op jit(solution)/shard_map/reduce_scatter | solution.py:327
  758.6 607.3 %all-reduce.14.cloned.1.call-start = ((), (), s32[]{:S(2)}) async-start(), calls=%async_computation.8 | async-start | bytes 7077888 | tf_op jit(solution)/shard_map/psum | solution.py:340
  758.7 217.6 %copy-start.50 = (f32[3072]{0:T(1024)S(1)}, f32[3072]{0:T(1024)}, u32[]{:S(2)}) copy-start(f32[3072]{0:T(1024)} %get-tuple-element.696) | copy-start | bytes 36868
  758.7 217.6 %copy-start.54 = (f32[768]{0:T(1024)S(1)}, f32[768]{0:T(1024)}, u32[]{:S(2)}) copy-start(f32[768]{0:T(1024)} %get-tuple-element.700) | copy-start | bytes 9220
  758.8 217.6 %copy-start.57 = (f32[768]{0:T(1024)S(1)}, f32[768]{0:T(1024)}, u32[]{:S(2)}) copy-start(f32[768]{0:T(1024)} %get-tuple-element.699) | copy-start | bytes 9220
  758.8 217.6 %copy-start.60 = (f32[768]{0:T(1024)S(1)}, f32[768]{0:T(1024)}, u32[]{:S(2)}) copy-start(f32[768]{0:T(1024)} %get-tuple-element.698) | copy-start | bytes 9220
  758.8 217.6 %copy-start.63 = (f32[768]{0:T(1024)S(1)}, f32[768]{0:T(1024)}, u32[]{:S(2)}) copy-start(f32[768]{0:T(1024)} %get-tuple-element.694) | copy-start | bytes 9220
  758.8 217.6 %copy-start.66 = (f32[768]{0:T(1024)S(1)}, f32[768]{0:T(1024)}, u32[]{:S(2)}) copy-start(f32[768]{0:T(1024)} %get-tuple-element.693) | copy-start | bytes 9220
  758.8 217.6 %copy-start.69 = (f32[768]{0:T(1024)S(1)}, f32[768]{0:T(1024)}, u32[]{:S(2)}) copy-start(f32[768]{0:T(1024)} %get-tuple-element.692) | copy-start | bytes 9220
  758.8 217.6 %copy-start.72 = (f32[768]{0:T(1024)S(1)}, f32[768]{0:T(1024)}, u32[]{:S(2)}) copy-start(f32[768]{0:T(1024)} %get-tuple-element.690) | copy-start | bytes 9220
  758.8 217.6 %copy-start.75 = (f32[768]{0:T(1024)S(1)}, f32[768]{0:T(1024)}, u32[]{:S(2)}) copy-start(f32[768]{0:T(1024)} %get-tuple-element.689) | copy-start | bytes 9220
  812.8 14.5 %collective-permute-start = (bf16[532,768]{1,0:T(8,128)(2,1)S(1)}, bf16[532,768]{1,0:T(8,128)(2,1)S(1)}, u32[]{:S(2)}, u32[]{:S(2)}) collective-permute-start(bf16[532,768]{1,0:T(8,128)(2,1)S(1)} %add_convert_fusion.10), channel_id=1, source_target_pairs={{0,2},{1,3},{4,6},{5,7},{8,10},{9,11},{12,14},{13,15},{16,18},{17,... | collective-permute-start | bytes 2451464 | tf_op jit(solution)/shard_map/while/body/eval_jaxpr/ppermute | solution.py:15
  881.4 16.3 %collective-permute-start = (bf16[532,768]{1,0:T(8,128)(2,1)S(1)}, bf16[532,768]{1,0:T(8,128)(2,1)S(1)}, u32[]{:S(2)}, u32[]{:S(2)}) collective-permute-start(bf16[532,768]{1,0:T(8,128)(2,1)S(1)} %add_convert_fusion.10), channel_id=1, source_target_pairs={{0,2},{1,3},{4,6},{5,7},{8,10},{9,11},{12,14},{13,15},{16,18},{17,... | collective-permute-start | bytes 2451464 | tf_op jit(solution)/shard_map/while/body/eval_jaxpr/ppermute | solution.py:15
  951.7 16.2 %collective-permute-start = (bf16[532,768]{1,0:T(8,128)(2,1)S(1)}, bf16[532,768]{1,0:T(8,128)(2,1)S(1)}, u32[]{:S(2)}, u32[]{:S(2)}) collective-permute-start(bf16[532,768]{1,0:T(8,128)(2,1)S(1)} %add_convert_fusion.10), channel_id=1, source_target_pairs={{0,2},{1,3},{4,6},{5,7},{8,10},{9,11},{12,14},{13,15},{16,18},{17,... | collective-permute-start | bytes 2451464 | tf_op jit(solution)/shard_map/while/body/eval_jaxpr/ppermute | solution.py:15
  968.9 333.9 %collective-permute-start.5 = (bf16[1,80,768]{2,1,0:T(8,128)(2,1)S(1)}, bf16[1,80,768]{2,1,0:T(8,128)(2,1)S(1)}, u32[]{:S(2)}, u32[]{:S(2)}) collective-permute-start(bf16[1,80,768]{2,1,0:T(8,128)(2,1)S(1)} %slice.70), channel_id=1, source_target_pairs={{2,0},{3,1},{6,4},{7,5},{10,8},{11,9},{14,12},{15,13},{18,16},{19,... | collective-permute-start | bytes 368648 | tf_op jit(solution)/shard_map/ppermute | solution.py:15
  971.8 332.6 %collective-permute-start.7 = (bf16[1,532,768]{2,1,0:T(8,128)(2,1)S(1)}, bf16[1,532,768]{2,1,0:T(8,128)(2,1)S(1)}, u32[]{:S(2)}, u32[]{:S(2)}) collective-permute-start(bf16[1,532,768]{2,1,0:T(8,128)(2,1)S(1)} %slice.115), channel_id=1, source_target_pairs={{0,2},{1,3},{4,6},{5,7},{8,10},{9,11},{12,14},{13,15},{16,18},{17,... | collective-permute-start | bytes 2451464 | tf_op jit(solution)/shard_map/ppermute | solution.py:15
  1306.0 68.7 %copy-start.1 = (bf16[2,768,768]{2,1,0:T(8,128)(2,1)S(1)}, bf16[2,768,768]{2,1,0:T(8,128)(2,1)}, u32[]{:S(2)}) copy-start(bf16[2,768,768]{2,1,0:T(8,128)(2,1)} %param.25) | copy-start | bytes 7077892
  (188 other events, 1272.9 us)
Sparse Core Ops, SparseCore 0:
  755.1 69.9 reduce-scatter.6
  828.8 128.4 reduce-scatter.4
  960.9 162.6 reduce-scatter.8
  1127.0 161.2 reduce-scatter.10
  1291.8 73.9 all-reduce.13
where the time goes:
time: 1390 us; the launch traced here: 1380 us
  matrix products  653 us (47%)
  waiting for transfers between devices  420 us (30%)
  local copies, waits for them, and re-layouts  92.2 us (7%)
  other arithmetic  85.1 us (6%)
  blocking collectives  47.4 us (3%)
  loops' own time  34.8 us (3%)
  starting transfers between devices  33.2 us (2%)
  between operations  16 us (1%)
    reduce_scatter x1, waiting for transfers between devices, local(): lax.psum_scatter(totals[9], 'dp', scatter_dimension=0, tiled=True)  162 us
    dot_general x9, matrix products, layer_pieces(): jnp.dot(activated, down_weight, preferred_element_type=jnp.float32)  149 us
    reduce_scatter x1, waiting for transfers between devices, local(): lax.psum_scatter(totals[7], 'dp', scatter_dimension=0, tiled=True)  102 us
    ppermute x14, waiting for transfers between devices, from_behind(): lax.ppermute(value, axis, [(source, source + steps) for source in range(l...  97.1 us
    sub x9, matrix products, layer_pieces(): softmax_out = jax.nn.softmax(scores, axis=-1)  83.8 us
    dot_general x9, matrix products, layer_pieces(): jnp.einsum('hqk,khd->qhd', softmax_low, value_rows, preferred_element_typ...  68.2 us
    dot_general x3, matrix products, layer_pieces(): jnp.dot(first_low, up_weight, preferred_element_type=jnp.float32) + up_bias  63 us
    psum x1, waiting for transfers between devices, local(): lax.psum(slots[0].astype(jnp.bfloat16), 'section').astype(jnp.float32)  57 us
  transfers between devices with their start and end apart: 19, of which 13 were waited for; matrix products, arithmetic and copies ran while one was open for 17% of the time, Pallas kernels for 0%

commit v1 on v0

v1 whole, which is shorter than its diff:
```python
import jax
import jax.numpy as jnp
from jax import lax
from jax.sharding import PartitionSpec as P

HEAD_DIM = 64
EPS = 1e-06
BF = jnp.bfloat16
F32 = jnp.float32


def dot(left, right, left_dim=1, right_dim=0):
    return lax.dot_general(
        left, right, (((left_dim,), (right_dim,)), ((), ())), preferred_element_type=F32
    )


def norm_parts(resid):
    centre = jnp.mean(resid, -1, keepdims=True)
    offset = resid - centre
    spread = jnp.mean(offset * offset, -1, keepdims=True)
    scale = lax.rsqrt(spread + EPS)
    return offset * scale, scale


def norm_back(grad, normed, scale, gain):
    inner = grad * gain
    mean_inner = jnp.mean(inner, -1, keepdims=True)
    mean_prod = jnp.mean(inner * normed, -1, keepdims=True)
    d_resid = scale * (inner - mean_inner - normed * mean_prod)
    return d_resid, jnp.sum(grad * normed, 0), jnp.sum(grad, 0)


def gelu_pair(pre):
    cdf = 0.5 * lax.erfc(-pre * (0.5**0.5))
    density = jnp.exp(-0.5 * pre * pre) * ((0.5 / jnp.pi) ** 0.5)
    return pre * cdf, cdf + pre * density


def heads_of(rows):
    return rows.reshape(rows.shape[0], -1, HEAD_DIM)


def attention_forward(queries, keys, values):
    scores = (
        jnp.einsum("qhd,khd->hqk", heads_of(queries), heads_of(keys), preferred_element_type=F32)
        * HEAD_DIM**-0.5
    )
    probs = jax.nn.softmax(scores, axis=-1)
    attended = jnp.einsum(
        "hqk,khd->qhd", probs.astype(BF), heads_of(values), preferred_element_type=F32
    )
    return probs, attended.reshape(queries.shape).astype(BF)


def attention_backward(queries, keys, values, probs, d_attended):
    scale = HEAD_DIM**-0.5
    d_att = heads_of(d_attended)
    d_probs = jnp.einsum("qhd,khd->hqk", d_att, heads_of(values), preferred_element_type=F32)
    d_values = jnp.einsum("hqk,qhd->khd", probs.astype(BF), d_att, preferred_element_type=F32)
    row_terms = jnp.sum(probs * d_probs, -1, keepdims=True)
    d_scores = (probs * (d_probs - row_terms)).astype(BF)
    d_queries = jnp.einsum("hqk,khd->qhd", d_scores, heads_of(keys), preferred_element_type=F32)
    d_keys = jnp.einsum("hqk,qhd->khd", d_scores, heads_of(queries), preferred_element_type=F32)
    return (
        (d_queries * scale).reshape(queries.shape).astype(BF),
        (d_keys * scale).reshape(keys.shape).astype(BF),
        d_values.reshape(values.shape).astype(BF),
    )


def tail_forward(hidden, attended, par):
    first_sum = hidden.astype(F32) + (dot(attended, par["out_weight"]) + par["out_bias"])
    normed1, scale1 = norm_parts(first_sum)
    first_norm = normed1 * par["norm1_gain"] + par["norm1_shift"]
    first_low = first_norm.astype(BF)
    up_pre = dot(first_low, par["up_weight"]) + par["up_bias"]
    act, slope = gelu_pair(up_pre)
    act = act.astype(BF)
    second_sum = first_norm + (dot(act, par["down_weight"]) + par["down_bias"])
    normed2, scale2 = norm_parts(second_sum)
    layer_out = normed2 * par["norm2_gain"] + par["norm2_shift"]
    return layer_out.astype(BF), (normed1, scale1, first_low, slope.astype(BF), act, normed2, scale2)


def tail_backward(grad_out, attended, saved, par):
    normed1, scale1, first_low, slope, act, normed2, scale2 = saved
    d_second, g_gain2, g_shift2 = norm_back(grad_out, normed2, scale2, par["norm2_gain"])
    d_down = d_second.astype(BF)
    d_up = (slope.astype(F32) * dot(d_down, par["down_weight"], 1, 1)).astype(BF)
    d_first_norm = d_second + dot(d_up, par["up_weight"], 1, 1)
    d_first, g_gain1, g_shift1 = norm_back(d_first_norm, normed1, scale1, par["norm1_gain"])
    d_branch = d_first.astype(BF)
    d_attended = dot(d_branch, par["out_weight"], 1, 1).astype(BF)
    small = {
        "norm2_gain": g_gain2,
        "norm2_shift": g_shift2,
        "down_bias": jnp.sum(d_down.astype(F32), 0),
        "up_bias": jnp.sum(d_up.astype(F32), 0),
        "norm1_gain": g_gain1,
        "norm1_shift": g_shift1,
        "out_bias": jnp.sum(d_branch.astype(F32), 0),
    }
    g_down = dot(act, d_down, 0, 0).astype(BF)
    g_up = dot(first_low, d_up, 0, 0).astype(BF)
    g_out = dot(attended, d_branch, 0, 0).astype(BF)
    return d_first, d_attended, (g_down, g_up, g_out), small


NAMES = (
    "qkv_weight",
    "query_bias",
    "value_bias",
    "out_weight",
    "out_bias",
    "norm1_gain",
    "norm1_shift",
    "up_weight",
    "up_bias",
    "down_weight",
    "down_bias",
    "norm2_gain",
    "norm2_shift",
)
SMALL = tuple(name for name in NAMES if not name.endswith("weight"))


def swap(value, axis, bit):
    size = lax.axis_size(axis)
    return lax.ppermute(value, axis, [(i, i ^ bit) for i in range(size)])


def bit_of(axis, bit):
    return (lax.axis_index(axis) // bit) % 2


def halve(value, axis, bit, dim):
    mine = bit_of(axis, bit)
    kept = lax.dynamic_index_in_dim(value, mine, dim, keepdims=False)
    sent = lax.dynamic_index_in_dim(value, 1 - mine, dim, keepdims=False)
    got = swap(sent, axis, bit)
    return (kept.astype(F32) + got.astype(F32)).astype(value.dtype)


def double(value, axis, bit, dim):
    got = swap(value, axis, bit)
    mine = bit_of(axis, bit)
    low = jnp.where(mine == 0, value, got)
    high = jnp.where(mine == 0, got, value)
    return jnp.stack([low, high], dim)


def reduce_blocks(grad):
    blocks = lax.axis_size("dp")
    rows, columns = grad.shape
    part = rows // blocks
    value = halve(grad.reshape(rows, 2, columns // 2), "section", 1, 1)
    value = value.reshape(blocks, 2, part // 2, columns // 2)
    value = halve(value, "section", 2, 1)
    bit = 1
    while bit < blocks:
        left = value.shape[0]
        value = halve(value.reshape(left // 2, 2, part // 2, columns // 2), "dp", bit, 1)
        bit *= 2
    value = value.reshape(part // 2, columns // 2)
    value = double(value, "section", 2, 0).reshape(part, columns // 2)
    return double(value, "section", 1, 1).reshape(part, columns)


def side_by_side(grad, blocks):
    rows, columns = grad.shape
    return grad.reshape(blocks, 4, rows // (4 * blocks), columns).swapaxes(1, 2).reshape(rows // 4, 4 * columns)


def one_above_another(block, columns):
    rows = block.shape[0]
    return block.reshape(rows, 4, columns).swapaxes(0, 1).reshape(4 * rows, columns)


def reduce_small(vectors):
    blocks = lax.axis_size("dp")
    packed = jnp.concatenate([v.reshape(blocks, -1) for v in vectors], 1)
    packed = packed + swap(packed, "section", 1)
    packed = packed + swap(packed, "section", 2)
    bit = 1
    while bit < blocks:
        packed = halve(packed.reshape(packed.shape[0] // 2, 2, -1), "dp", bit, 1)
        bit *= 2
    packed = packed.reshape(-1)
    pieces, at = [], 0
    for v in vectors:
        width = v.shape[0] // blocks
        pieces.append(packed[at : at + width])
        at += width
    return pieces


def local(inputs, *rest):
    weights = dict(zip(NAMES, rest[: len(NAMES)]))
    cotangent, masked_rows, row_valid = (value[0] for value in rest[len(NAMES) :])
    params = []
    for layer in range(2):
        params.append(
            {
                name: stacked[layer] if stacked.ndim == 3 else stacked[layer].astype(F32)
                for name, stacked in weights.items()
            }
        )
    par0, par1 = params
    hidden = inputs[0]
    rows, width = hidden.shape
    blocks = lax.axis_size("dp")

    projected = dot(hidden, par0["qkv_weight"])
    q0 = (projected[:, :width] + par0["query_bias"]).astype(BF)
    k0 = projected[:, width : 2 * width].astype(BF)
    v0 = (projected[:, 2 * width :] + par0["value_bias"]).astype(BF)
    probs0, att0 = attention_forward(q0, k0, v0)
    boundary, saved0 = tail_forward(hidden, att0, par0)

    pick = (masked_rows[:, None] == jnp.arange(rows, dtype=jnp.int32)).astype(BF)
    valid = row_valid.astype(F32)[:, None]
    slots = dot(pick, boundary).astype(BF)
    key_value = dot(boundary, par1["qkv_weight"][:, width:])
    q1 = (dot(slots, par1["qkv_weight"][:, :width]) + par1["query_bias"]).astype(BF)
    k1 = key_value[:, :width].astype(BF)
    v1 = (key_value[:, width:] + par1["value_bias"]).astype(BF)
    probs1, att1 = attention_forward(q1, k1, v1)
    top, saved1 = tail_forward(slots, att1, par1)
    masked_out = (top.astype(F32) * valid).astype(BF)

    top_grad = cotangent.astype(F32) * valid
    d_first1, d_att1, big1, small1 = tail_backward(top_grad, att1, saved1, par1)
    down1, up1, out1 = big1
    ff1 = reduce_blocks(jnp.concatenate([up1, side_by_side(down1, blocks)], 1))
    d_q1, d_k1, d_v1 = attention_backward(q1, k1, v1, probs1, d_att1)
    small1["query_bias"] = jnp.sum(d_q1.astype(F32), 0)
    small1["value_bias"] = jnp.sum(d_v1.astype(F32), 0)
    d_kv1 = jnp.concatenate([d_k1, d_v1], 1)
    qkv1 = jnp.concatenate([dot(slots, d_q1, 0, 0), dot(boundary, d_kv1, 0, 0)], 1).astype(BF)
    at1 = reduce_blocks(jnp.concatenate([qkv1, out1], 1))
    d_slots = d_first1 + dot(d_q1, par1["qkv_weight"][:, :width], 1, 1)
    slots_hi = d_slots.astype(BF)
    slots_lo = (d_slots - slots_hi.astype(F32)).astype(BF)
    d_boundary = (
        dot(d_kv1, par1["qkv_weight"][:, width:], 1, 1)
        + dot(pick, slots_hi, 0, 0)
        + dot(pick, slots_lo, 0, 0)
    )
    bound_grad = d_boundary.astype(BF).astype(F32)

    d_first0, d_att0, big0, small0 = tail_backward(bound_grad, att0, saved0, par0)
    down0, up0, out0 = big0
    ff0 = reduce_blocks(jnp.concatenate([up0, side_by_side(down0, blocks)], 1))
    d_q0, d_k0, d_v0 = attention_backward(q0, k0, v0, probs0, d_att0)
    small0["query_bias"] = jnp.sum(d_q0.astype(F32), 0)
    small0["value_bias"] = jnp.sum(d_v0.astype(F32), 0)
    d_proj0 = jnp.concatenate([d_q0, d_k0, d_v0], 1)
    qkv0 = dot(hidden, d_proj0, 0, 0).astype(BF)
    at0 = reduce_blocks(jnp.concatenate([qkv0, out0], 1))
    input_grad = d_first0 + dot(d_proj0, par0["qkv_weight"], 1, 1)

    vectors = reduce_small([small[name] for small in (small0, small1) for name in SMALL])
    count = len(SMALL)
    result = {name: jnp.stack([vectors[i], vectors[count + i]]) for i, name in enumerate(SMALL)}
    ff_width = par0["up_weight"].shape[1]
    result["up_weight"] = jnp.stack([ff[:, :ff_width] for ff in (ff0, ff1)]).astype(F32)
    result["down_weight"] = jnp.stack(
        [one_above_another(ff[:, ff_width:], width) for ff in (ff0, ff1)]
    ).astype(F32)
    result["qkv_weight"] = jnp.stack([at[:, : 3 * width] for at in (at0, at1)]).astype(F32)
    result["out_weight"] = jnp.stack([at[:, 3 * width :] for at in (at0, at1)]).astype(F32)
    return (masked_out[None], input_grad[None]) + tuple(result[name] for name in NAMES)


def solution(mesh):
    both = ("dp", "section")
    wide, flat = P(None, "dp", None), P(None, "dp")
    return jax.shard_map(
        local,
        mesh=mesh,
        in_specs=(P(both, None, None),)
        + (P(),) * len(NAMES)
        + (P(both, None, None), P(both, None), P(both, None)),
        out_specs=(P(both, None, None), P(both, None, None))
        + tuple(wide if name.endswith("weight") else flat for name in NAMES),
        check_vma=False,
    )
```

time: 1390 us -> 623 us (0.45)
  matrix products: 653 us -> 164 us
  waiting for transfers between devices: 420 us -> 231 us
  blocking collectives: 47.4 us -> 0 us
  loops' own time: 34.8 us -> 0 us
  local copies, waits for them, and re-layouts: 92.2 us -> 111 us
    dot_general x81 -> x40, matrix products: 569 us -> 152 us  [the longest x30 105 us: dot(): lax.dot_general(left, right, (((left_dim,), (right_dim,)), ((), ())), pre...]
    reduce_scatter x4 -> x0, waiting for transfers between devices: 264 us -> none  [the longest x1 162 us: local(): lax.psum_scatter(totals[9], 'dp', scatter_dimension=0, tiled=True)]
    ppermute x14 -> x33, waiting for transfers between devices: 97.1 us -> 231 us  [swap(): return lax.ppermute(value, axis, [(i, i ^ bit) for i in range(size)])]
    sub x9 -> x2, matrix products: 83.8 us -> 11.8 us  [attention_forward(): probs = jax.nn.softmax(scores, axis=-1)]
    psum x1 -> x0, waiting for transfers between devices: 57 us -> none  [local(): lax.psum(slots[0].astype(jnp.bfloat16), 'section').astype(jnp.float32)]
    unnamed x1 -> x0, blocking collectives: 40.9 us -> none
    another operation x2 -> x0, loops' own time: 34.8 us -> none  [the longest x1 30.4 us: local(): lax.scan(backward_tick, (start_rows, zero_totals), tick_list)]
    reshape x0 -> x29, local copies, waits for them, and re-layouts: none -> 29.5 us  [the longest x2 13.9 us: side_by_side(): grad.reshape(blocks, 4, rows // (4 * blocks), columns).swapaxes(1, 2)]
  transfers between devices with their start and end apart: 19 -> 33, of which waited for: 13 -> 13; matrix products, arithmetic and copies ran while one was open for 17% -> 30% of each run, Pallas kernels for 0% -> 0%
where the time goes in v1:
time: 623 us; the launch traced here: 615 us
  waiting for transfers between devices  231 us (37%)
  matrix products  164 us (26%)
  local copies, waits for them, and re-layouts  111 us (18%)
  other arithmetic  83 us (13%)
  starting transfers between devices  23.1 us (4%)
    ppermute x33, waiting for transfers between devices, swap(): return lax.ppermute(value, axis, [(i, i ^ bit) for i in range(size)])  231 us
    dot_general x30, matrix products, dot(): lax.dot_general(left, right, (((left_dim,), (right_dim,)), ((), ())), pre...  105 us
    convert_element_type x16, other arithmetic, halve(): return (kept.astype(F32) + got.astype(F32)).astype(value.dtype)  26.2 us
    ppermute x33, starting transfers between devices, swap(): return lax.ppermute(value, axis, [(i, i ^ bit) for i in range(size)])  23.1 us
    unnamed x221, local copies, waits for them, and re-layouts  19.9 us
    dot_general x2, matrix products, attention_backward(): jnp.einsum('qhd,khd->hqk', d_att, heads_of(values), preferred_element_typ...  17.3 us
    dynamic_slice x4, local copies, waits for them, and re-layouts, halve(): kept = lax.dynamic_index_in_dim(value, mine, dim, keepdims=False)  15.4 us
    reshape x2, local copies, waits for them, and re-layouts, side_by_side(): grad.reshape(blocks, 4, rows // (4 * blocks), columns).swapaxes(1, 2)  13.9 us
  transfers between devices with their start and end apart: 33, of which 13 were waited for; matrix products, arithmetic and copies ran while one was open for 30% of the time, Pallas kernels for 0%

profile of v1, /device:TPU:0, one launch (start us, length us, event | category | flops | bytes accessed | tf_op | source)
XLA Modules:
  0.0 615.5 jit_solution(16466882422252438569)
XLA Ops:
  0.7 4.2 slice_bitcast_fusion
  6.0 3.3 fusion.65
  12.5 1.8 copy.123
  14.4 8.5 %fusion.221 = (f32[12,532]{1,0:T(8,128)S(1)}, f32[12,532,532]{1,2,0:T(8,128)}) fusion(bf16[532,12,64]{0,2,1:T(8,128)(2,1)S(1)} %bitcast.435, bf16[532,12,64]{0,2,1:T(8,128)(2,1)S(1)} %bitcast.422), kind=kOutput, calls=%fused_computation.423 | convolution fusion | flops 444914240 | bytes 15244992 | tf_op jit(solution)/shard_map/sub | solution.py:49
  22.9 7.6 %fusion.101 = bf16[12,64,532]{2,1,0:T(8,128)(2,1)S(1)} fusion(bf16[532,12,64]{0,2,1:T(8,128)(2,1)S(1)} %bitcast.461, f32[12,532,532]{1,2,0:T(8,128)} %get-tuple-element.169, f32[12,532]{1,0:T(8,128)S(1)} %get-tuple-element.168), kind=kOutput, calls=%fused_computation.182 | convolution fusion | flops 441926016 | bytes 15244992 | tf_op jit(solution)/shard_map/hqk,khd->qhd/dot_general | solution.py:50
  33.4 21.6 %multiply_convert_fusion.2 = (bf16[532,3072]{1,0:T(8,128)(2,1)S(1)}, f32[532,3072]{1,0:T(8,128)}, f32[532,3072]{1,0:T(8,128)}) fusion(f32[3072]{0:T(1024)S(1)} %bitcast.474, bf16[2,768,3072]{2,1,0:T(8,128)(2,1)} %param.25, f32[532,768]{1,0:T(8,128)S(1)} %get-tuple-element.171, f32[768]{0:T(1024)S(1)} %get-tuple-element.100, ...), kind=kOutput, calls=%fused_computation.32 | convolution fusion | flops 2620197888 | bytes 22718624 | tf_op jit(solution)/shard_map/dot_general | solution.py:13
  55.2 3.0 fusion.223
  72.2 3.3 fusion.224
  75.5 2.8 convolution_convert_fusion.11
  79.1 4.7 multiply_convert_fusion.7
  87.4 3.9 convert_reduce_fusion.7
  91.3 2.2 multiply_reduce_fusion.9
  95.6 2.8 multiply_reduce_fusion.2
  103.7 1.8 fusion.90
  107.7 8.9 %convert_reduce_fusion = (f32[3072]{0:T(1024)S(1)}, bf16[532,3072]{1,0:T(8,128)(2,1)}) fusion(bf16[2,3072,768]{2,1,0:T(8,128)(2,1)S(1)} %bitcast.485, f32[532,768]{1,0:T(8,128)S(1)} %get-tuple-element.112, f32[532,3072]{1,0:T(8,128)} %get-tuple-element.116, f32[532,3072]{1,0:T(8,128)} %get-tuple-element.172, f32[3072]{0:T(1024)S(1)} %bitcast.475), kind=kOutput, calls=%fused_computation.30 | convolution fusion | flops 2530308096 | bytes 22732800 | tf_op jit(solution)/shard_map/dot_general | solution.py:13
  116.6 6.6 %multiply_reduce_fusion.4 = (f32[768]{0:T(1024)S(1)}, f32[532]{0:T(1024)S(1)}, f32[532]{0:T(1024)S(1)}, f32[768]{0:T(1024)S(1)}, f32[532,768]{1,0:T(8,128)S(1)}) fusion(f32[532,768]{1,0:T(8,128)S(1)} %copy-done.4, f32[532]{0:T(1024)S(1)} %copy-done.51, f32[532]{0:T(1024)S(1)} %broadcast_multiply_fusion.5, f32[768]{0:T(1024)S(1)} %copy-done.49, ...), kind=kOutput, calls=%fused_computation.162 | convolution fusion | flops 2514374144 | bytes 12932416 | tf_op jit(solution)/shard_map/dot_general | solution.py:13
  125.2 1.8 convolution_convert_fusion.10
  127.0 2.2 copy.131
  129.2 14.5 %multiply_reduce_fusion = (f32[12,532]{1,0:T(8,128)S(1)}, f32[12,532,532]{1,2,0:T(8,128)}) fusion(f32[12,532,532]{1,2,0:T(8,128)} %get-tuple-element.169, f32[12,532]{1,0:T(8,128)S(1)} %get-tuple-element.168, bf16[532,12,64]{0,2,1:T(8,128)(2,1)} %bitcast.465, bf16[532,12,64]{0,2,1:T(8,128)(2,1)S(1)} %bitcast.462), kind=kOutput, calls=%fused_computation.3 | convolution fusion | flops 444907328 | bytes 28855680 | tf_op jit(solution)/shard_map/qhd,khd->hqk/dot_general | solution.py:59
  143.7 9.4 %convert_reduce_fusion.3 = (f32[12,64]{1,0:T(8,128)S(1)}, bf16[12,64,532]{2,1,0:T(8,128)(2,1)}) fusion(bf16[532,12,64]{0,2,1:T(8,128)(2,1)S(1)} %bitcast.466, f32[12,532,532]{1,2,0:T(8,128)} %get-tuple-element.169, f32[12,532]{1,0:T(8,128)S(1)} %get-tuple-element.168), kind=kOutput, calls=%fused_computation.144 | convolution fusion | flops 442742400 | bytes 15248064 | tf_op jit(solution)/shard_map/hqk,qhd->khd/dot_general | solution.py:60
  153.1 11.3 %multiply_convert_fusion = bf16[12,532,532]{1,2,0:T(8,128)(2,1)S(1)} fusion(f32[12,532,532]{1,2,0:T(8,128)} %get-tuple-element.189, f32[12,532]{1,0:T(8,128)S(1)} %get-tuple-element.188, f32[12,532,532]{1,2,0:T(8,128)} %get-tuple-element.169, f32[12,532]{1,0:T(8,128)S(1)} %get-tuple-element.168), kind=kLoop, calls=%fused_computation.2 | loop fusion | flops 13585152 | bytes 34013952 | tf_op jit(solution)/shard_map/convert_element_type | solution.py:62
  164.5 1.8 convert_reduce_fusion.4
  170.1 8.2 %fusion.49 = bf16[768,1,3072]{2,0,1:T(8,128)(2,1)} fusion(bf16[532,3072]{1,0:T(8,128)(2,1)} %get-tuple-element.195, f32[532,768]{1,0:T(8,128)S(1)} %copy-done.4, f32[768]{0:T(1024)S(1)} %copy-done.75, f32[768]{0:T(1024)S(1)} %copy-done.49, f32[532]{0:T(1024)S(1)} %copy-done.51, f32[532]{0:T(1024)S(1)} %broadcast_multiply_fusion.5), kind=kOutput, calls=%fused_computation.88 | convolution fusion | flops 2514693120 | bytes 9631904 | tf_op jit(solution)/shard_map/dot_general | solution.py:13
  178.2 5.6 convolution_convert_fusion.2
  183.8 8.1 %copy.191 = bf16[8,4,96,768]{3,1,2,0:T(4,128)(2,1)} copy(bf16[8,4,96,768]{3,2,1,0:T(8,128)(2,1)} %bitcast.424) | data formatting | bytes 9437184 | tf_op jit(solution)/shard_map/reshape | solution.py:172
  191.9 9.5 %concatenate.40 = bf16[768,1,3072]{2,0,1:T(8,128)(2,1)} reshape(bf16[8,96,4,768]{3,2,1,0:T(4,128)(2,1)} %bitcast.402) | data formatting | bytes 9437184 | tf_op jit(solution)/shard_map/concatenate | solution.py:254
  201.5 6.2 %fusion.26 = bf16[768,3072]{1,0:T(8,128)(2,1)} fusion(s32[]{:T(128)S(6)} %select_n.278, bf16[768,1,3072]{2,0,1:T(8,128)(2,1)} %fusion.49, bf16[768,1,3072]{2,0,1:T(8,128)(2,1)} %concatenate.40), kind=kLoop, calls=%fused_computation.57 | loop fusion | flops 2359296 | bytes 14155780 | tf_op jit(solution)/shard_map/jit(dynamic_index_in_dim)/squeeze | solution.py:140
  207.7 3.6 fusion.50
  212.7 5.8 copy.190
  218.5 9.7 %concatenate.43 = bf16[768,1,3072]{2,0,1:T(8,128)(2,1)} reshape(bf16[8,96,4,768]{3,2,1,0:T(4,128)(2,1)} %bitcast.403) | data formatting | bytes 9437184 | tf_op jit(solution)/shard_map/concatenate | solution.py:235
  228.2 6.2 %fusion.22 = bf16[768,3072]{1,0:T(8,128)(2,1)} fusion(s32[]{:T(128)S(6)} %select_n.278, bf16[768,1,3072]{2,0,1:T(8,128)(2,1)} %fusion.50, bf16[768,1,3072]{2,0,1:T(8,128)(2,1)} %concatenate.43), kind=kLoop, calls=%fused_computation.53 | loop fusion | flops 2359296 | bytes 14155780 | tf_op jit(solution)/shard_map/jit(dynamic_index_in_dim)/squeeze | solution.py:140
  234.9 7.2 %multiply_convert_fusion.4 = bf16[12,64,532]{2,1,0:T(8,128)(2,1)} fusion(bf16[532,12,64]{0,2,1:T(8,128)(2,1)S(1)} %bitcast.436, bf16[12,532,532]{1,2,0:T(8,128)(2,1)} %copy-done), kind=kOutput, calls=%fused_computation.146 | convolution fusion | flops 435542016 | bytes 8426880 | tf_op jit(solution)/shard_map/hqk,qhd->khd/dot_general | solution.py:64
  243.3 4.4 fusion.48
  248.0 1.7 constant_dynamic-slice_fusion.13
  249.7 4.3 copy.136
  254.2 5.1 convolution_convert_fusion.5
  261.3 2.8 collective-permute-start.15
  265.6 2.4 copy.141
  274.9 3.9 pad_maximum_fusion.1
  278.8 11.8 %reshape.458 = bf16[768,2,1536]{2,1,0:T(2,128)(2,1)} reshape(bf16[768,3072]{1,0:T(8,128)(2,1)} %pad_maximum_fusion.1) | data formatting | bytes 9437184 | tf_op jit(solution)/shard_map/reshape | solution.py:157
  293.1 12.0 %constant_dynamic-slice_fusion.10 = (bf16[768,1,1536]{2,1,0:T(2,128)(2,1)}, bf16[768,1,1536]{2,1,0:T(2,128)(2,1)S(1)}) fusion(bf16[768,2,1536]{2,1,0:T(2,128)(2,1)} %reshape.458, s32[]{:T(128)S(6)} %select_n.277, s32[]{:T(128)S(6)} %select_n.278), kind=kLoop, calls=%fused_computation.356 | loop fusion | bytes 9437192 | tf_op jit(solution)/shard_map/jit(dynamic_index_in_dim)/dynamic_slice | solution.py:139
  305.2 2.0 copy.192
  307.2 2.6 collective-permute-start.18
  309.9 6.8 %add_bitcast_fusion = f32[1,532,768]{2,1,0:T(8,128)} fusion(f32[532,768]{1,0:T(8,128)} %copy-done.27, bf16[2,768,2304]{2,1,0:T(8,128)(2,1)} %param.18, bf16[532,768]{0,1:T(8,128)(2,1)} %bitcast.489, bf16[532,768]{0,1:T(8,128)(2,1)} %bitcast.468, bf16[532,768]{0,1:T(8,128)(2,1)S(1)} %bitcast.453), kind=kOutput, calls=%fused_computation.164 | convolution fusion | flops 1890481152 | bytes 9603072 | tf_op jit(solution)/shard_map/dot_general | solution.py:13
  316.7 2.6 copy.166
  319.3 4.4 copy.156
  327.9 2.6 fusion.32
  331.4 2.6 fusion.31
  336.6 22.8 %collective-permute-done.1 = bf16[8,48,1536]{2,1,0:T(8,128)(2,1)S(1)} collective-permute-done((bf16[8,48,1536]{2,1,0:T(8,128)(2,1)S(1)}, bf16[8,48,1536]{2,1,0:T(8,128)(2,1)S(1)}, u32[]{:S(2)}, u32[]{:S(2)}) %collective-permute-start.1) | collective-permute-done | bytes 1179680 | tf_op jit(solution)/shard_map/ppermute | solution.py:130
  360.4 23.6 %collective-permute-done.8 = bf16[8,48,1536]{2,1,0:T(8,128)(2,1)S(1)} collective-permute-done((bf16[8,48,1536]{2,1,0:T(8,128)(2,1)S(1)}, bf16[8,48,1536]{2,1,0:T(8,128)(2,1)S(1)}, u32[]{:S(2)}, u32[]{:S(2)}) %collective-permute-start.8) | collective-permute-done | bytes 1179680 | tf_op jit(solution)/shard_map/ppermute | solution.py:130
  385.7 13.4 %collective-permute-done.9 = bf16[4,48,1536]{2,1,0:T(8,128)(2,1)S(1)} collective-permute-done((bf16[4,48,1536]{2,1,0:T(8,128)(2,1)S(1)}, bf16[4,48,1536]{2,1,0:T(8,128)(2,1)S(1)}, u32[]{:S(2)}, u32[]{:S(2)}) %collective-permute-start.9) | collective-permute-done | bytes 589856 | tf_op jit(solution)/shard_map/ppermute | solution.py:130
  400.3 9.6 %collective-permute-done.10 = bf16[2,48,1536]{2,1,0:T(8,128)(2,1)S(1)} collective-permute-done((bf16[2,48,1536]{2,1,0:T(8,128)(2,1)S(1)}, bf16[2,48,1536]{2,1,0:T(8,128)(2,1)S(1)}, u32[]{:S(2)}, u32[]{:S(2)}) %collective-permute-start.10) | collective-permute-done | bytes 294944 | tf_op jit(solution)/shard_map/ppermute | solution.py:130
  411.0 6.6 %collective-permute-done.11 = bf16[1,48,1536]{2,1,0:T(8,128)(2,1)S(1)} collective-permute-done((bf16[1,48,1536]{2,1,0:T(8,128)(2,1)S(1)}, bf16[1,48,1536]{2,1,0:T(8,128)(2,1)S(1)}, u32[]{:S(2)}, u32[]{:S(2)}) %collective-permute-start.11) | collective-permute-done | bytes 147488 | tf_op jit(solution)/shard_map/ppermute | solution.py:130
  418.7 4.2 collective-permute-done.12
  423.7 9.4 %fusion.6 = bf16[768,3072]{1,0:T(8,128)(2,1)} fusion(bf16[768,3072]{1,0:T(8,128)(2,1)} %collective-permute-done.19, s32[]{:T(128)S(6)} %select_n.277, bf16[768,1,3072]{2,0,1:T(8,128)(2,1)} %fusion.49, bf16[768,1,3072]{2,0,1:T(8,128)(2,1)S(1)} %bitcast.397), kind=kLoop, calls=%fused_computation.20 | loop fusion | flops 11796480 | bytes 18874372 | tf_op jit(solution)/shard_map/convert_element_type | solution.py:142
  433.1 3.2 dynamic-slice_bitcast_fusion.1
  437.1 5.9 fusion.5
  448.4 42.4 %collective-permute-done.20 = bf16[8,48,3072]{2,1,0:T(8,128)(2,1)} collective-permute-done((bf16[8,48,3072]{2,1,0:T(8,128)(2,1)}, bf16[8,48,3072]{2,1,0:T(8,128)(2,1)}, u32[]{:S(2)}, u32[]{:S(2)}) %collective-permute-start.20) | collective-permute-done | bytes 2359328 | tf_op jit(solution)/shard_map/ppermute | solution.py:130
  490.8 2.6 fusion.30
  494.0 45.2 %collective-permute-done.27 = bf16[8,48,3072]{2,1,0:T(8,128)(2,1)S(1)} collective-permute-done((bf16[8,48,3072]{2,1,0:T(8,128)(2,1)S(1)}, bf16[8,48,3072]{2,1,0:T(8,128)(2,1)S(1)}, u32[]{:S(2)}, u32[]{:S(2)}) %collective-permute-start.27) | collective-permute-done | bytes 2359328 | tf_op jit(solution)/shard_map/ppermute | solution.py:130
  542.2 24.1 %collective-permute-done.28 = bf16[4,48,3072]{2,1,0:T(8,128)(2,1)S(1)} collective-permute-done((bf16[4,48,3072]{2,1,0:T(8,128)(2,1)S(1)}, bf16[4,48,3072]{2,1,0:T(8,128)(2,1)S(1)}, u32[]{:S(2)}, u32[]{:S(2)}) %collective-permute-start.28) | collective-permute-done | bytes 1179680 | tf_op jit(solution)/shard_map/ppermute | solution.py:130
  568.4 17.1 %collective-permute-done.29 = bf16[2,48,3072]{2,1,0:T(8,128)(2,1)S(1)} collective-permute-done((bf16[2,48,3072]{2,1,0:T(8,128)(2,1)S(1)}, bf16[2,48,3072]{2,1,0:T(8,128)(2,1)S(1)}, u32[]{:S(2)}, u32[]{:S(2)}) %collective-permute-start.29) | collective-permute-done | bytes 589856 | tf_op jit(solution)/shard_map/ppermute | solution.py:130
  586.8 13.0 %collective-permute-done.30 = bf16[1,48,3072]{2,1,0:T(8,128)(2,1)S(1)} collective-permute-done((bf16[1,48,3072]{2,1,0:T(8,128)(2,1)S(1)}, bf16[1,48,3072]{2,1,0:T(8,128)(2,1)S(1)}, u32[]{:S(2)}, u32[]{:S(2)}) %collective-permute-start.30) | collective-permute-done | bytes 294944 | tf_op jit(solution)/shard_map/ppermute | solution.py:130
  600.9 7.9 %collective-permute-done.31 = bf16[48,3072]{1,0:T(8,128)(2,1)S(1)} collective-permute-done((bf16[48,3072]{1,0:T(8,128)(2,1)S(1)}, bf16[48,3072]{1,0:T(8,128)(2,1)S(1)}, u32[]{:S(2)}, u32[]{:S(2)}) %collective-permute-start.31) | collective-permute-done | bytes 294944 | tf_op jit(solution)/shard_map/ppermute | solution.py:130
  (444 shorter events, 91.1 us)
Async XLA Ops:
  11.8 11.0 %copy-start.11 = (bf16[532,768]{0,1:T(8,128)(2,1)}, bf16[532,768]{0,1:T(8,128)(2,1)S(1)}, u32[]{:S(2)}) copy-start(bf16[532,768]{0,1:T(8,128)(2,1)S(1)} %copy.124) | copy-start | bytes 2451460
  12.5 10.4 %copy-start.7 = (bf16[532,768]{0,1:T(8,128)(2,1)}, bf16[532,768]{0,1:T(8,128)(2,1)S(1)}, u32[]{:S(2)}) copy-start(bf16[532,768]{0,1:T(8,128)(2,1)S(1)} %copy.125) | copy-start | bytes 2451460
  14.3 8.5 %copy-start.35 = (bf16[532,768]{0,1:T(8,128)(2,1)}, bf16[532,768]{0,1:T(8,128)(2,1)S(1)}, u32[]{:S(2)}) copy-start(bf16[532,768]{0,1:T(8,128)(2,1)S(1)} %copy.123) | copy-start | bytes 2451460
  30.5 24.6 %slice-start.8 = ((s8[9437184]{0:T(1024)(128)(4,1)}), s8[1048576]{0:T(1024)(128)(4,1)S(1)}, s32[]{:S(2)}) async-start(s8[9437184]{0:T(1024)(128)(4,1)} %bitcast.480), calls=%async_computation.8 | async-start | bytes 2097152
  31.6 23.5 %copy-start.3 = (f32[532,768]{1,0:T(8,128)}, f32[532,768]{1,0:T(8,128)S(1)}, u32[]{:S(2)}) copy-start(f32[532,768]{1,0:T(8,128)S(1)} %get-tuple-element.171) | copy-start | bytes 4902916
  31.9 23.2 %copy-start.50 = (f32[532]{0:T(1024)}, f32[532]{0:T(1024)S(1)}, u32[]{:S(2)}) copy-start(f32[532]{0:T(1024)S(1)} %add_rsqrt_fusion.1) | copy-start | bytes 6388
  32.7 22.4 %copy-start.65 = (f32[1,3072]{1,0:T(1,128)}, f32[1,3072]{1,0:T(1,128)S(1)}, u32[]{:S(2)}) copy-start(f32[1,3072]{1,0:T(1,128)S(1)} %get-tuple-element.148) | copy-start | bytes 36868
  33.4 21.7 %copy-start.48 = (f32[768]{0:T(1024)}, f32[768]{0:T(1024)S(1)}, u32[]{:S(2)}) copy-start(f32[768]{0:T(1024)S(1)} %get-tuple-element.204) | copy-start | bytes 9220
  33.4 21.7 %copy-start.74 = (f32[768]{0:T(1024)}, f32[768]{0:T(1024)S(1)}, u32[]{:S(2)}) copy-start(f32[768]{0:T(1024)S(1)} %get-tuple-element.100) | copy-start | bytes 9220
  33.4 21.8 %slice-start.9 = ((s8[9437184]{0:T(1024)(128)(4,1)}), s8[4194304]{0:T(1024)(128)(4,1)S(1)}, s32[]{:S(2)}) async-start(s8[9437184]{0:T(1024)(128)(4,1)} %bitcast.480), calls=%async_computation.9 | async-start | bytes 8388608
  33.4 21.7 %slice-start.10 = ((s8[9437184]{0:T(1024)(128)(4,1)}), s8[4194304]{0:T(1024)(128)(4,1)S(1)}, s32[]{:S(2)}) async-start(s8[9437184]{0:T(1024)(128)(4,1)} %bitcast.480), calls=%async_computation.10 | async-start | bytes 8388608
  75.5 8.3 %slice-start.11 = ((s8[9437184]{0:T(1024)(128)(4,1)}), s8[4194304]{0:T(1024)(128)(4,1)S(1)}, s32[]{:S(2)}) async-start(s8[9437184]{0:T(1024)(128)(4,1)} %bitcast.482), calls=%async_computation.11 | async-start | bytes 8388608
  78.8 14.7 %copy-start.68 = (f32[80]{0:T(128)}, f32[80]{0:T(128)S(1)}, u32[]{:S(2)}) copy-start(f32[80]{0:T(128)S(1)} %broadcast_multiply_fusion.11) | copy-start | bytes 964
  79.0 14.5 %copy-start.72 = (f32[80]{0:T(128)}, f32[80]{0:T(128)S(1)}, u32[]{:S(2)}) copy-start(f32[80]{0:T(128)S(1)} %add_rsqrt_fusion.3) | copy-start | bytes 964
  107.4 9.2 %copy-start.29 = (f32[532,768]{1,0:T(8,128)}, f32[532,768]{1,0:T(8,128)S(1)}, u32[]{:S(2)}) copy-start(f32[532,768]{1,0:T(8,128)S(1)} %get-tuple-element.112) | copy-start | bytes 4902916
  107.7 8.9 %copy-start.4 = (f32[532,768]{1,0:T(8,128)S(1)}, f32[532,768]{1,0:T(8,128)}, u32[]{:S(2)}) copy-start(f32[532,768]{1,0:T(8,128)} %copy-done.3) | copy-start | bytes 4902916
  107.7 8.9 %copy-start.49 = (f32[768]{0:T(1024)S(1)}, f32[768]{0:T(1024)}, u32[]{:S(2)}) copy-start(f32[768]{0:T(1024)} %copy-done.48) | copy-start | bytes 9220
  107.7 8.9 %copy-start.51 = (f32[532]{0:T(1024)S(1)}, f32[532]{0:T(1024)}, u32[]{:S(2)}) copy-start(f32[532]{0:T(1024)} %copy-done.50) | copy-start | bytes 6388
  129.2 14.5 %copy-start.37 = (bf16[532,768]{0,1:T(8,128)(2,1)S(1)}, bf16[532,768]{0,1:T(8,128)(2,1)}, u32[]{:S(2)}) copy-start(bf16[532,768]{0,1:T(8,128)(2,1)} %copy.131) | copy-start | bytes 2451460
  153.1 11.3 %copy-start.8 = (bf16[532,768]{0,1:T(8,128)(2,1)S(1)}, bf16[532,768]{0,1:T(8,128)(2,1)}, u32[]{:S(2)}) copy-start(bf16[532,768]{0,1:T(8,128)(2,1)} %copy-done.7) | copy-start | bytes 2451460
  167.6 75.6 %copy-start.18 = (bf16[12,64,532]{2,1,0:T(8,128)(2,1)}, bf16[12,64,532]{2,1,0:T(8,128)(2,1)S(1)}, u32[]{:S(2)}) copy-start(bf16[12,64,532]{2,1,0:T(8,128)(2,1)S(1)} %get-tuple-element.191) | copy-start | bytes 2451460
  169.6 90.2 %collective-permute-start.14 = (f32[8,2304]{1,0:T(8,128)}, f32[8,2304]{1,0:T(8,128)}, u32[]{:S(2)}, u32[]{:S(2)}) collective-permute-start(f32[8,2304]{1,0:T(8,128)} %concatenate.38), channel_id=1, source_target_pairs={{0,1},{1,0},{2,3},{3,2},{4,5},{5,4},{6,7},{7,6},{8,9},{9,8},{10,11... | collective-permute-start | bytes 221192 | tf_op jit(solution)/shard_map/ppermute | solution.py:130
  207.7 216.0 %collective-permute-start.19 = (bf16[768,3072]{1,0:T(8,128)(2,1)}, bf16[768,3072]{1,0:T(8,128)(2,1)}, u32[]{:S(2)}, u32[]{:S(2)}) collective-permute-start(bf16[768,3072]{1,0:T(8,128)(2,1)} %fusion.26), channel_id=1, source_target_pairs={{0,1},{1,0},{2,3},{3,2},{4,5},{5,4},{6,7},{7,6},{8,9},{9,8},{10,11... | collective-permute-start | bytes 14155784 | tf_op jit(solution)/shard_map/ppermute | solution.py:130
  234.4 202.7 %collective-permute-start.26 = (bf16[768,3072]{1,0:T(8,128)(2,1)}, bf16[768,3072]{1,0:T(8,128)(2,1)}, u32[]{:S(2)}, u32[]{:S(2)}) collective-permute-start(bf16[768,3072]{1,0:T(8,128)(2,1)} %fusion.22), channel_id=1, source_target_pairs={{0,1},{1,0},{2,3},{3,2},{4,5},{5,4},{6,7},{7,6},{8,9},{9,8},{10,11... | collective-permute-start | bytes 14155784 | tf_op jit(solution)/shard_map/ppermute | solution.py:130
  254.1 10.1 %copy-start.24 = (bf16[12,64,80]{2,1,0:T(8,128)(2,1)S(1)}, bf16[12,64,80]{2,1,0:T(8,128)(2,1)}, u32[]{:S(2)}) copy-start(bf16[12,64,80]{2,1,0:T(8,128)(2,1)} %copy-done.23) | copy-start | bytes 368644
  254.1 10.1 %copy-start.33 = (bf16[80,768]{1,0:T(8,128)(2,1)S(1)}, bf16[80,768]{1,0:T(8,128)(2,1)}, u32[]{:S(2)}) copy-start(bf16[80,768]{1,0:T(8,128)(2,1)} %copy-done.31) | copy-start | bytes 368644
  254.1 73.8 %collective-permute-start = (bf16[768,1536]{1,0:T(8,128)(2,1)}, bf16[768,1536]{1,0:T(8,128)(2,1)}, u32[]{:S(2)}, u32[]{:S(2)}) collective-permute-start(bf16[768,1536]{1,0:T(8,128)(2,1)} %bitcast.441), channel_id=1, source_target_pairs={{0,1},{1,0},{2,3},{3,2},{4,5},{5,4},{6,7},{7,6},{8,9},{9,8},{10,11... | collective-permute-start | bytes 7077896 | tf_op jit(solution)/shard_map/ppermute | solution.py:130
  261.3 6.7 %collective-permute-start.15 = (f32[8,2304]{1,0:T(8,128)}, f32[8,2304]{1,0:T(8,128)}, u32[]{:S(2)}, u32[]{:S(2)}) collective-permute-start(f32[8,2304]{1,0:T(8,128)} %add.553), channel_id=1, source_target_pairs={{0,2},{1,3},{2,0},{3,1},{4,6},{5,7},{6,4},{7,5},{8,10},{9,11},{10,... | collective-permute-start | bytes 221192 | tf_op jit(solution)/shard_map/ppermute | solution.py:130
  273.4 17.2 %collective-permute-start.16 = (f32[4,2304]{1,0:T(4,128)}, f32[4,2304]{1,0:T(4,128)}, u32[]{:S(2)}, u32[]{:S(2)}) collective-permute-start(f32[4,2304]{1,0:T(4,128)} %bitcast.394), channel_id=1, source_target_pairs={{0,4},{4,0},{8,12},{12,8},{16,20},{20,16},{24,28},{28,24},{1,5},{5... | collective-permute-start | bytes 110600 | tf_op jit(solution)/shard_map/ppermute | solution.py:130
  278.8 11.8 %copy-start.44 = (f32[4,1,2304]{2,1,0:T(1,128)S(1)}, f32[4,1,2304]{2,1,0:T(1,128)}, u32[]{:S(2)}) copy-start(f32[4,1,2304]{2,1,0:T(1,128)} %get-tuple-element.144) | copy-start | bytes 110596
  291.5 15.7 %collective-permute-start.17 = (f32[2,2304]{1,0:T(2,128)S(1)}, f32[2,2304]{1,0:T(2,128)S(1)}, u32[]{:S(2)}, u32[]{:S(2)}) collective-permute-start(f32[2,2304]{1,0:T(2,128)S(1)} %bitcast.473), channel_id=1, source_target_pairs={{0,8},{4,12},{8,0},{12,4},{16,24},{20,28},{24,16},{28,20},{1,9},{5... | collective-permute-start | bytes 55304 | tf_op jit(solution)/shard_map/ppermute | solution.py:130
  307.2 24.2 %collective-permute-start.7 = (bf16[768,1536]{1,0:T(8,128)(2,1)}, bf16[768,1536]{1,0:T(8,128)(2,1)}, u32[]{:S(2)}, u32[]{:S(2)}) collective-permute-start(bf16[768,1536]{1,0:T(8,128)(2,1)} %bitcast.393), channel_id=1, source_target_pairs={{0,1},{1,0},{2,3},{3,2},{4,5},{5,4},{6,7},{7,6},{8,9},{9,8},{10,11... | collective-permute-start | bytes 7077896 | tf_op jit(solution)/shard_map/ppermute | solution.py:130
  307.2 16.5 %collective-permute-start.18 = (f32[1,2304]{1,0:T(1,128)S(1)}, f32[1,2304]{1,0:T(1,128)S(1)}, u32[]{:S(2)}, u32[]{:S(2)}) collective-permute-start(f32[1,2304]{1,0:T(1,128)S(1)} %constant_dynamic-slice_fusion.2), channel_id=1, source_target_pairs={{0,16},{4,20},{8,24},{12,28},{16,0},{20,4},{24,8},{28,12},{1,17},{... | collective-permute-start | bytes 27656 | tf_op jit(solution)/shard_map/ppermute | solution.py:130
  319.3 8.5 %copy-start.2 = (bf16[768,1,1536]{2,0,1:T(8,128)(2,1)S(1)}, bf16[768,1,1536]{2,0,1:T(8,128)(2,1)}, u32[]{:S(2)}) copy-start(bf16[768,1,1536]{2,0,1:T(8,128)(2,1)} %copy.166) | copy-start | bytes 7077892
  330.5 28.9 %collective-permute-start.1 = (bf16[8,48,1536]{2,1,0:T(8,128)(2,1)S(1)}, bf16[8,48,1536]{2,1,0:T(8,128)(2,1)S(1)}, u32[]{:S(2)}, u32[]{:S(2)}) collective-permute-start(bf16[8,48,1536]{2,1,0:T(8,128)(2,1)S(1)} %dynamic-slice_bitcast_fusion.5), channel_id=1, source_target_pairs={{0,2},{1,3},{2,0},{3,1},{4,6},{5,7},{6,4},{7,5},{8,10},{9,11},{10,... | collective-permute-start | bytes 3538952 | tf_op jit(solution)/shard_map/ppermute | solution.py:130
  334.1 49.9 %collective-permute-start.8 = (bf16[8,48,1536]{2,1,0:T(8,128)(2,1)S(1)}, bf16[8,48,1536]{2,1,0:T(8,128)(2,1)S(1)}, u32[]{:S(2)}, u32[]{:S(2)}) collective-permute-start(bf16[8,48,1536]{2,1,0:T(8,128)(2,1)S(1)} %dynamic-slice_bitcast_fusion.4), channel_id=1, source_target_pairs={{0,2},{1,3},{2,0},{3,1},{4,6},{5,7},{6,4},{7,5},{8,10},{9,11},{10,... | collective-permute-start | bytes 3538952 | tf_op jit(solution)/shard_map/ppermute | solution.py:130
  359.8 25.1 %collective-permute-start.2 = (bf16[4,48,1536]{2,1,0:T(8,128)(2,1)S(1)}, bf16[4,48,1536]{2,1,0:T(8,128)(2,1)S(1)}, u32[]{:S(2)}, u32[]{:S(2)}) collective-permute-start(bf16[4,48,1536]{2,1,0:T(8,128)(2,1)S(1)} %dynamic-slice_bitcast_fusion.9), channel_id=1, source_target_pairs={{0,4},{4,0},{8,12},{12,8},{16,20},{20,16},{24,28},{28,24},{1,5},{5... | collective-permute-start | bytes 1769480 | tf_op jit(solution)/shard_map/ppermute | solution.py:130
  384.0 39.7 %slice-start = ((s8[4718592]{0:T(1024)(128)(4,1)}), s8[4194304]{0:T(1024)(128)(4,1)S(1)}, s32[]{:S(2)}) async-start(s8[4718592]{0:T(1024)(128)(4,1)} %bitcast.396), calls=%async_computation | async-start | bytes 8388608
  384.4 14.7 %collective-permute-start.9 = (bf16[4,48,1536]{2,1,0:T(8,128)(2,1)S(1)}, bf16[4,48,1536]{2,1,0:T(8,128)(2,1)S(1)}, u32[]{:S(2)}, u32[]{:S(2)}) collective-permute-start(bf16[4,48,1536]{2,1,0:T(8,128)(2,1)S(1)} %dynamic-slice_bitcast_fusion.8), channel_id=1, source_target_pairs={{0,4},{4,0},{8,12},{12,8},{16,20},{20,16},{24,28},{28,24},{1,5},{5... | collective-permute-start | bytes 1769480 | tf_op jit(solution)/shard_map/ppermute | solution.py:130
  385.1 38.5 %slice-start.1 = ((s8[4718592]{0:T(1024)(128)(4,1)}), s8[524288]{0:T(1024)(128)(4,1)S(1)}, s32[]{:S(2)}) async-start(s8[4718592]{0:T(1024)(128)(4,1)} %bitcast.396), calls=%async_computation.1 | async-start | bytes 1048576
  385.2 14.6 %collective-permute-start.3 = (bf16[2,48,1536]{2,1,0:T(8,128)(2,1)S(1)}, bf16[2,48,1536]{2,1,0:T(8,128)(2,1)S(1)}, u32[]{:S(2)}, u32[]{:S(2)}) collective-permute-start(bf16[2,48,1536]{2,1,0:T(8,128)(2,1)S(1)} %dynamic-slice_bitcast_fusion.11), channel_id=1, source_target_pairs={{0,8},{4,12},{8,0},{12,4},{16,24},{20,28},{24,16},{28,20},{1,9},{5... | collective-permute-start | bytes 884744 | tf_op jit(solution)/shard_map/ppermute | solution.py:130
  399.2 10.7 %collective-permute-start.10 = (bf16[2,48,1536]{2,1,0:T(8,128)(2,1)S(1)}, bf16[2,48,1536]{2,1,0:T(8,128)(2,1)S(1)}, u32[]{:S(2)}, u32[]{:S(2)}) collective-permute-start(bf16[2,48,1536]{2,1,0:T(8,128)(2,1)S(1)} %dynamic-slice_bitcast_fusion.10), channel_id=1, source_target_pairs={{0,8},{4,12},{8,0},{12,4},{16,24},{20,28},{24,16},{28,20},{1,9},{5... | collective-permute-start | bytes 884744 | tf_op jit(solution)/shard_map/ppermute | solution.py:130
  399.9 10.2 %collective-permute-start.4 = (bf16[1,48,1536]{2,1,0:T(8,128)(2,1)S(1)}, bf16[1,48,1536]{2,1,0:T(8,128)(2,1)S(1)}, u32[]{:S(2)}, u32[]{:S(2)}) collective-permute-start(bf16[1,48,1536]{2,1,0:T(8,128)(2,1)S(1)} %constant_dynamic-slice_fusion.11), channel_id=1, source_target_pairs={{0,16},{4,20},{8,24},{12,28},{16,0},{20,4},{24,8},{28,12},{1,17},{... | collective-permute-start | bytes 442376 | tf_op jit(solution)/shard_map/ppermute | solution.py:130
  410.0 7.6 %collective-permute-start.11 = (bf16[1,48,1536]{2,1,0:T(8,128)(2,1)S(1)}, bf16[1,48,1536]{2,1,0:T(8,128)(2,1)S(1)}, u32[]{:S(2)}, u32[]{:S(2)}) collective-permute-start(bf16[1,48,1536]{2,1,0:T(8,128)(2,1)S(1)} %constant_dynamic-slice_fusion.8), channel_id=1, source_target_pairs={{0,16},{4,20},{8,24},{12,28},{16,0},{20,4},{24,8},{28,12},{1,17},{... | collective-permute-start | bytes 442376 | tf_op jit(solution)/shard_map/ppermute | solution.py:130
  410.1 8.4 %collective-permute-start.5 = (bf16[48,1536]{1,0:T(8,128)(2,1)S(1)}, bf16[48,1536]{1,0:T(8,128)(2,1)S(1)}, u32[]{:S(2)}, u32[]{:S(2)}) collective-permute-start(bf16[48,1536]{1,0:T(8,128)(2,1)S(1)} %fusion.187), channel_id=1, source_target_pairs={{0,2},{1,3},{2,0},{3,1},{4,6},{5,7},{6,4},{7,5},{8,10},{9,11},{10,... | collective-permute-start | bytes 442376 | tf_op jit(solution)/shard_map/ppermute | solution.py:130
  417.7 5.2 collective-permute-start.12
  418.6 26.0 %collective-permute-start.6 = (bf16[96,1536]{1,0:T(8,128)(2,1)S(1)}, bf16[96,1536]{1,0:T(8,128)(2,1)}, u32[]{:S(2)}, u32[]{:S(2)}) collective-permute-start(bf16[96,1536]{1,0:T(8,128)(2,1)S(1)} %bitcast.458), channel_id=1, source_target_pairs={{0,1},{1,0},{2,3},{3,2},{4,5},{5,4},{6,7},{7,6},{8,9},{9,8},{10,11... | collective-permute-start | bytes 884744 | tf_op jit(solution)/shard_map/ppermute | solution.py:130
  423.6 13.5 %slice-start.2 = ((s8[4718592]{0:T(1024)(128)(4,1)}), s8[4194304]{0:T(1024)(128)(4,1)S(1)}, s32[]{:S(2)}) async-start(s8[4718592]{0:T(1024)(128)(4,1)} %bitcast.398), calls=%async_computation.2 | async-start | bytes 8388608
  423.6 13.5 %slice-start.3 = ((s8[4718592]{0:T(1024)(128)(4,1)}), s8[524288]{0:T(1024)(128)(4,1)S(1)}, s32[]{:S(2)}) async-start(s8[4718592]{0:T(1024)(128)(4,1)} %bitcast.398), calls=%async_computation.3 | async-start | bytes 1048576
  423.6 22.0 %collective-permute-start.13 = (bf16[96,1536]{1,0:T(8,128)(2,1)}, bf16[96,1536]{1,0:T(8,128)(2,1)}, u32[]{:S(2)}, u32[]{:S(2)}) collective-permute-start(bf16[96,1536]{1,0:T(8,128)(2,1)} %bitcast.77), channel_id=1, source_target_pairs={{0,1},{1,0},{2,3},{3,2},{4,5},{5,4},{6,7},{7,6},{8,9},{9,8},{10,11... | collective-permute-start | bytes 884744 | tf_op jit(solution)/shard_map/ppermute | solution.py:130
  436.3 54.4 %collective-permute-start.20 = (bf16[8,48,3072]{2,1,0:T(8,128)(2,1)}, bf16[8,48,3072]{2,1,0:T(8,128)(2,1)}, u32[]{:S(2)}, u32[]{:S(2)}) collective-permute-start(bf16[8,48,3072]{2,1,0:T(8,128)(2,1)} %dynamic-slice_bitcast_fusion.1), channel_id=1, source_target_pairs={{0,2},{1,3},{2,0},{3,1},{4,6},{5,7},{6,4},{7,5},{8,10},{9,11},{10,... | collective-permute-start | bytes 7077896 | tf_op jit(solution)/shard_map/ppermute | solution.py:130
  443.1 47.7 %slice-start.4 = ((s8[4718592]{0:T(1024)(128)(4,1)}), s8[4194304]{0:T(1024)(128)(4,1)S(1)}, s32[]{:S(2)}) async-start(s8[4718592]{0:T(1024)(128)(4,1)} %bitcast.405), calls=%async_computation.4 | async-start | bytes 8388608
  443.2 96.0 %collective-permute-start.27 = (bf16[8,48,3072]{2,1,0:T(8,128)(2,1)S(1)}, bf16[8,48,3072]{2,1,0:T(8,128)(2,1)S(1)}, u32[]{:S(2)}, u32[]{:S(2)}) collective-permute-start(bf16[8,48,3072]{2,1,0:T(8,128)(2,1)S(1)} %dynamic-slice_bitcast_fusion), channel_id=1, source_target_pairs={{0,2},{1,3},{2,0},{3,1},{4,6},{5,7},{6,4},{7,5},{8,10},{9,11},{10,... | collective-permute-start | bytes 7077896 | tf_op jit(solution)/shard_map/ppermute | solution.py:130
  446.7 44.0 %slice-start.5 = ((s8[4718592]{0:T(1024)(128)(4,1)}), s8[524288]{0:T(1024)(128)(4,1)S(1)}, s32[]{:S(2)}) async-start(s8[4718592]{0:T(1024)(128)(4,1)} %bitcast.405), calls=%async_computation.5 | async-start | bytes 1048576
  493.5 48.1 %collective-permute-start.21 = (bf16[4,48,3072]{2,1,0:T(8,128)(2,1)S(1)}, bf16[4,48,3072]{2,1,0:T(8,128)(2,1)S(1)}, u32[]{:S(2)}, u32[]{:S(2)}) collective-permute-start(bf16[4,48,3072]{2,1,0:T(8,128)(2,1)S(1)} %dynamic-slice_bitcast_fusion.3), channel_id=1, source_target_pairs={{0,4},{4,0},{8,12},{12,8},{16,20},{20,16},{24,28},{28,24},{1,5},{5... | collective-permute-start | bytes 3538952 | tf_op jit(solution)/shard_map/ppermute | solution.py:130
  540.2 26.0 %collective-permute-start.28 = (bf16[4,48,3072]{2,1,0:T(8,128)(2,1)S(1)}, bf16[4,48,3072]{2,1,0:T(8,128)(2,1)S(1)}, u32[]{:S(2)}, u32[]{:S(2)}) collective-permute-start(bf16[4,48,3072]{2,1,0:T(8,128)(2,1)S(1)} %dynamic-slice_bitcast_fusion.2), channel_id=1, source_target_pairs={{0,4},{4,0},{8,12},{12,8},{16,20},{20,16},{24,28},{28,24},{1,5},{5... | collective-permute-start | bytes 3538952 | tf_op jit(solution)/shard_map/ppermute | solution.py:130
  542.1 24.7 %collective-permute-start.22 = (bf16[2,48,3072]{2,1,0:T(8,128)(2,1)S(1)}, bf16[2,48,3072]{2,1,0:T(8,128)(2,1)S(1)}, u32[]{:S(2)}, u32[]{:S(2)}) collective-permute-start(bf16[2,48,3072]{2,1,0:T(8,128)(2,1)S(1)} %dynamic-slice_bitcast_fusion.7), channel_id=1, source_target_pairs={{0,8},{4,12},{8,0},{12,4},{16,24},{20,28},{24,16},{28,20},{1,9},{5... | collective-permute-start | bytes 1769480 | tf_op jit(solution)/shard_map/ppermute | solution.py:130
  566.7 18.9 %collective-permute-start.29 = (bf16[2,48,3072]{2,1,0:T(8,128)(2,1)S(1)}, bf16[2,48,3072]{2,1,0:T(8,128)(2,1)S(1)}, u32[]{:S(2)}, u32[]{:S(2)}) collective-permute-start(bf16[2,48,3072]{2,1,0:T(8,128)(2,1)S(1)} %dynamic-slice_bitcast_fusion.6), channel_id=1, source_target_pairs={{0,8},{4,12},{8,0},{12,4},{16,24},{20,28},{24,16},{28,20},{1,9},{5... | collective-permute-start | bytes 1769480 | tf_op jit(solution)/shard_map/ppermute | solution.py:130
  567.0 18.9 %collective-permute-start.23 = (bf16[1,48,3072]{2,1,0:T(8,128)(2,1)S(1)}, bf16[1,48,3072]{2,1,0:T(8,128)(2,1)S(1)}, u32[]{:S(2)}, u32[]{:S(2)}) collective-permute-start(bf16[1,48,3072]{2,1,0:T(8,128)(2,1)S(1)} %constant_dynamic-slice_fusion.1), channel_id=1, source_target_pairs={{0,16},{4,20},{8,24},{12,28},{16,0},{20,4},{24,8},{28,12},{1,17},{... | collective-permute-start | bytes 884744 | tf_op jit(solution)/shard_map/ppermute | solution.py:130
  585.7 14.0 %collective-permute-start.30 = (bf16[1,48,3072]{2,1,0:T(8,128)(2,1)S(1)}, bf16[1,48,3072]{2,1,0:T(8,128)(2,1)S(1)}, u32[]{:S(2)}, u32[]{:S(2)}) collective-permute-start(bf16[1,48,3072]{2,1,0:T(8,128)(2,1)S(1)} %constant_dynamic-slice_fusion), channel_id=1, source_target_pairs={{0,16},{4,20},{8,24},{12,28},{16,0},{20,4},{24,8},{28,12},{1,17},{... | collective-permute-start | bytes 884744 | tf_op jit(solution)/shard_map/ppermute | solution.py:130
  585.9 14.8 %collective-permute-start.24 = (bf16[48,3072]{1,0:T(8,128)(2,1)S(1)}, bf16[48,3072]{1,0:T(8,128)(2,1)S(1)}, u32[]{:S(2)}, u32[]{:S(2)}) collective-permute-start(bf16[48,3072]{1,0:T(8,128)(2,1)S(1)} %fusion.171), channel_id=1, source_target_pairs={{0,2},{1,3},{2,0},{3,1},{4,6},{5,7},{6,4},{7,5},{8,10},{9,11},{10,... | collective-permute-start | bytes 884744 | tf_op jit(solution)/shard_map/ppermute | solution.py:130
  599.8 9.0 %collective-permute-start.31 = (bf16[48,3072]{1,0:T(8,128)(2,1)S(1)}, bf16[48,3072]{1,0:T(8,128)(2,1)S(1)}, u32[]{:S(2)}, u32[]{:S(2)}) collective-permute-start(bf16[48,3072]{1,0:T(8,128)(2,1)S(1)} %fusion.172), channel_id=1, source_target_pairs={{0,2},{1,3},{2,0},{3,1},{4,6},{5,7},{6,4},{7,5},{8,10},{9,11},{10,... | collective-permute-start | bytes 884744 | tf_op jit(solution)/shard_map/ppermute | solution.py:130
  600.8 8.2 %collective-permute-start.25 = (bf16[96,3072]{1,0:T(8,128)(2,1)S(1)}, bf16[96,3072]{1,0:T(8,128)(2,1)S(1)}, u32[]{:S(2)}, u32[]{:S(2)}) collective-permute-start(bf16[96,3072]{1,0:T(8,128)(2,1)S(1)} %bitcast.438), channel_id=1, source_target_pairs={{0,1},{1,0},{2,3},{3,2},{4,5},{5,4},{6,7},{7,6},{8,9},{9,8},{10,11... | collective-permute-start | bytes 1769480 | tf_op jit(solution)/shard_map/ppermute | solution.py:130
  608.9 2.1 collective-permute-start.32
  (77 other events, 289.6 us)
